TPU v7x, 512 devices: a whole 4x4x16 slice. The times are simulated.
512 devices in a mesh: depth: 32 (over y, z_hi, core), chan: 16 (over z_lo, x).
Axes of the slice: x: 4, y: 4, z: 16 (z_hi: 4, z_lo: 4; z = z_hi * 4 + z_lo), core: 2. Of those that a mesh axis runs over, the one named last changes fastest.
Arguments:
- grad_out: bfloat16 [128, 32, 32, 128], P('chan', 'depth'), may hold values from -6 to 6
- volume: bfloat16 [64, 64, 64, 256], P('chan', 'depth'), may hold values from -6 to 6
- weight: bfloat16 [27, 64, 128], replicated, may hold values from -0.15625 to 0.15625
Outputs:
- input_grad: bfloat16 [64, 64, 64, 256], P('chan', 'depth')
- weight_grad: float32 [27, 64, 128], P(None, 'chan', 'depth')
All inputs are finite; a program needn't handle non-finite values.
Results may differ from a plain program's by a relative error of at most 0.001.
Values may be sent and summed in bfloat16 or wider, within the bound.
A program may use at most 128 MiB of HBM per device.

v0:
```python
import math

import jax
import jax.numpy as jnp
from jax import lax
from jax.sharding import PartitionSpec as P


def from_behind(shard, axis, by):
    count = lax.axis_size(axis)
    pairs = [(i, i + by) for i in range(count) if 0 <= i + by < count]
    return lax.ppermute(shard, axis, pairs)


def upsample(stacked, axis, extended):
    tap_zero, tap_one, tap_two = (stacked[0], stacked[1], stacked[2])
    coord_axis = axis - 1
    length = tap_zero.shape[coord_axis]
    if extended:
        outer = length - 1
        even_cells = lax.slice_in_dim(tap_one, 0, outer, axis=coord_axis)
        odd_cells = lax.slice_in_dim(tap_zero, 1, length, axis=coord_axis) + lax.slice_in_dim(
            tap_two, 0, outer, axis=coord_axis
        )
    else:
        outer = length
        shifted = lax.slice_in_dim(tap_zero, 1, length, axis=coord_axis)
        shifted = jnp.concatenate(
            [shifted, jnp.zeros_like(lax.slice_in_dim(tap_zero, 0, 1, axis=coord_axis))],
            axis=coord_axis,
        )
        even_cells = tap_one
        odd_cells = shifted + tap_two
    paired = jnp.stack([even_cells, odd_cells], axis=coord_axis + 1)
    new_shape = list(even_cells.shape)
    new_shape[coord_axis] = 2 * outer
    return paired.reshape(new_shape)


def phase_grads(weight_rows, grads_ext):
    local_in = weight_rows.shape[0] // 27
    channels_out, planes, rows, cols = grads_ext.shape
    taps_out = jnp.dot(
        weight_rows, grads_ext.reshape(channels_out, -1), preferred_element_type=jnp.float32
    )
    taps_out = taps_out.reshape(3, 3, 3, local_in, planes, rows, cols)
    along_w = upsample(jnp.moveaxis(taps_out, 2, 0), 6, False)
    along_h = upsample(jnp.moveaxis(along_w, 1, 0), 4, False)
    return upsample(along_h, 2, True)


def weight_terms(inputs, grads_ext):
    row_extra = 0
    weight_cube = lax.conv_general_dilated(
        inputs[None],
        grads_ext[:, None],
        (1, 1, 1),
        ((1, 2), (1, row_extra), (1, 0)),
        rhs_dilation=(2, 2, 2),
        dimension_numbers=("CNDHW", "OIDHW", "NCDHW"),
        preferred_element_type=jnp.float32,
    )
    return jnp.transpose(weight_cube, (2, 3, 4, 0, 1)).reshape(
        27, weight_cube.shape[0], weight_cube.shape[1]
    )


def shards(grad_out, volume, weight):
    plane_next = from_behind(grad_out, "depth", -1)
    grads_ext = jnp.concatenate([grad_out, plane_next], axis=1)
    channels_out = weight.shape[2]
    local_in = volume.shape[0]
    every_channel = lax.all_gather(grads_ext, "chan", axis=0, tiled=True)
    own_weight = lax.dynamic_slice_in_dim(weight, lax.axis_index("chan") * local_in, local_in, 1)
    input_part = phase_grads(own_weight.reshape(27 * local_in, channels_out), every_channel)
    weight_part = weight_terms(volume, every_channel)
    input_grad = input_part.astype(jnp.bfloat16)
    summed = lax.psum_scatter(weight_part, "depth", scatter_dimension=2, tiled=True)
    cell_count = grad_out.shape[1] * lax.axis_size("depth") * grad_out.shape[2] * grad_out.shape[3]
    return (input_grad, summed * (1.0 / math.sqrt(cell_count)))


def solution(mesh):
    in_specs = (P("chan", "depth", None, None), P("chan", "depth", None, None), P())
    out_specs = (P("chan", "depth", None, None), P(None, "chan", "depth"))
    return jax.shard_map(shards, mesh=mesh, in_specs=in_specs, out_specs=out_specs, check_vma=False)
```

profile of v0, /device:TPU:1, one launch (start us, length us, event | category | flops | bytes accessed | tf_op | source)
XLA Modules:
  0.0 402.6 jit_solution(2060566481970177341)
XLA Ops:
  7.2 0.0 all-gather.2.cloned.1.call-start
  7.2 8.9 %collective-permute-start = (bf16[8,1,32,128]{3,2,1,0:T(8,128)(2,1)}, bf16[8,1,32,128]{3,2,1,0:T(8,128)(2,1)S(1)}, u32[]{:S(2)}, u32[]{:S(2)}) collective-permute-start(bf16[8,1,32,128]{3,2,1,0:T(8,128)(2,1)} %param.3), channel_id=1, source_target_pairs={{16,0},{32,16},{48,32},{64,48},{80,64},{96,80},{112,96},{128,112},... | collective-permute-start | bytes 196616 | tf_op jit(solution)/shard_map/ppermute | solution.py:12
  16.1 3.6 collective-permute-done
  19.7 1.5 pad_maximum_fusion.2
  21.2 0.0 all-gather.2.cloned.1.call-update
  21.2 20.5 %copy.63 = bf16[1,4,2,64,256]{1,0,4,3,2:T(2,128)(2,1)} copy(bf16[1,4,2,64,256]{4,3,2,1,0:T(8,128)(2,1)} %bitcast.80) | data formatting | bytes 524288 | tf_op jit(solution)/shard_map/broadcast_in_dim | solution.py:55
  41.8 1.3 dynamic-slice
  43.7 59.2 %all-gather.2.cloned.1.call-done = bf16[128,2,32,128]{3,2,1,0:T(8,128)(2,1)} async-done(((bf16[8,2,32,128]{3,2,1,0:T(8,128)(2,1)}), bf16[128,2,32,128]{3,2,1,0:T(8,128)(2,1)}) %all-gather.2.cloned.1.call-update) | async-done | bytes 2097168 | tf_op jit(solution)/shard_map/all_gather | solution.py:73
  102.9 3.5 copy.69
  106.4 0.7 fusion.4
  107.1 0.2 slice_bitcast_fusion.5
  107.3 0.7 slice.63
  108.0 0.4 fusion.8
  108.4 0.6 pad_maximum_fusion
  109.0 9.6 %copy.54 = f32[3,3,4,2,32,128,2]{4,6,5,3,2,1,0:T(2,128)} copy(f32[3,3,4,2,32,128,2]{5,2,4,3,1,0,6:T(4,128)S(1)} %pad_maximum_fusion) | data formatting | bytes 4718592 | tf_op jit(solution)/shard_map/stack | solution.py:34
  118.6 5.0 %slice_bitcast_fusion.2 = (f32[3,4,2,32,1,256]{3,5,2,1,0,4:T(8,128)}, f32[3,4,2,32,256]{3,4,2,1,0:T(8,128)S(1)}) fusion(f32[3,3,4,2,32,256]{4,5,3,2,0,1:T(8,128)} %bitcast.73), kind=kLoop, calls=%fused_computation.4 | loop fusion | bytes 3145728 | tf_op jit(solution)/shard_map/stack;squeeze | solution.py:34
  123.6 0.9 slice.67
  124.5 4.0 fusion.1
  128.5 2.3 copy.57
  130.8 2.3 copy.56
  133.2 0.1 fusion.9
  133.3 0.3 copy.58
  133.6 0.4 copy.59
  134.0 0.3 slice.74
  134.3 0.4 copy.61
  134.7 0.2 slice.75
  135.0 0.7 copy.66
  135.7 5.0 %copy.64 = bf16[128,1,2,32,128]{0,1,4,3,2:T(2,128)(2,1)} copy(bf16[128,1,2,32,128]{4,3,2,0,1:T(8,128)(2,1)S(1)} %bitcast.75) | data formatting | bytes 4194304 | tf_op jit(solution)/shard_map/broadcast_in_dim | solution.py:56
  140.7 83.3 %fusion.14 = f32[3,3,3,4,128]{4,3,2,1,0:T(4,128)S(1)} fusion(bf16[1,4,2,64,256]{1,0,4,3,2:T(2,128)(2,1)} %copy.63, bf16[128,1,2,32,128]{0,1,4,3,2:T(2,128)(2,1)} %copy.64), kind=kOutput, calls=%fused_computation.30 | convolution fusion | flops 111774720 | bytes 2414592 | tf_op jit(solution)/shard_map/transpose | solution.py:63
  224.0 0.1 copy.65
  224.1 171.0 %all-reduce.2 = f32[27,4,128]{0,2,1:T(8,128)S(1)} all-reduce(f32[27,4,128]{0,2,1:T(8,128)S(1)} %copy.65), channel_id=2, replica_groups=mesh['depth'=32,'chan'=16] {'depth'}, use_global_device_ids=true, to_apply=%region_0.0.clone | all-reduce | flops 13824 | bytes 110592
  395.1 0.6 dynamic-slice_multiply_fusion
  (9 shorter events, 0.2 us)
Async XLA Ops:
  7.2 36.5 %copy-start = (bf16[27,64,128]{2,1,0:T(8,128)(2,1)S(1)}, bf16[27,64,128]{2,1,0:T(8,128)(2,1)}, u32[]{:S(2)}) copy-start(bf16[27,64,128]{2,1,0:T(8,128)(2,1)} %param.5) | copy-start | bytes 1327108
  7.2 95.7 %all-gather.2.cloned.1.call-start = ((), (), s32[]{:S(2)}) async-start(), calls=%async_computation | async-start | bytes 2228224 | tf_op jit(solution)/shard_map/all_gather | solution.py:73
  7.2 12.5 %collective-permute-start = (bf16[8,1,32,128]{3,2,1,0:T(8,128)(2,1)}, bf16[8,1,32,128]{3,2,1,0:T(8,128)(2,1)S(1)}, u32[]{:S(2)}, u32[]{:S(2)}) collective-permute-start(bf16[8,1,32,128]{3,2,1,0:T(8,128)(2,1)} %param.3), channel_id=1, source_target_pairs={{16,0},{32,16},{48,32},{64,48},{80,64},{96,80},{112,96},{128,112},... | collective-permute-start | bytes 196616 | tf_op jit(solution)/shard_map/ppermute | solution.py:12
  133.3 2.4 copy-start.1
Sparse Core Ops, SparseCore 0:
  21.4 81.4 all-gather.1
where the time goes:
time: 411 us; the launch traced here: 403 us
  blocking collectives  171 us (42%)
  matrix products  84 us (20%)
  waiting for transfers between devices  62.8 us (15%)
  local copies, waits for them, and re-layouts  53.7 us (13%)
  between operations  14.9 us (4%)
  starting transfers between devices  8.92 us (2%)
  other arithmetic  7.28 us (2%)
    unnamed x1, blocking collectives  171 us
    transpose x1, matrix products, weight_terms(): jnp.transpose(weight_cube, (2, 3, 4, 0, 1))  83.3 us
    all_gather x1, waiting for transfers between devices, shards(): every_channel = lax.all_gather(grads_ext, 'chan', axis=0, tiled=True)  59.2 us
    broadcast_in_dim x1, local copies, waits for them, and re-layouts, weight_terms(): inputs[None]  20.5 us
    another operation x5, local copies, waits for them, and re-layouts, upsample(): paired = jnp.stack([even_cells, odd_cells], axis=coord_axis + 1)  19.5 us
    ppermute x1, starting transfers between devices, from_behind(): return lax.ppermute(shard, axis, pairs)  8.88 us
  transfers between devices with their start and end apart: 2, of which 2 were waited for; matrix products, arithmetic and copies ran while one was open for 5% of the time, Pallas kernels for 0%

commit v1 on v0

v1 whole, which is shorter than its diff:
```python
import math

import jax
import jax.numpy as jnp
from jax import lax
from jax.experimental import pallas as pl
from jax.experimental.pallas import tpu as pltpu
from jax.sharding import PartitionSpec as P

MESH = pl.DeviceIdType.MESH
BF16 = jnp.bfloat16
F32 = jnp.float32
NX, NY, NZ, NZL, DEPTH, CHAN = 4, 4, 16, 4, 32, 16
CI, ROWS, COLS = 4, 32, 128


def grid_of(shape):
    return lax.broadcasted_iota(jnp.int32, shape, 0), lax.broadcasted_iota(jnp.int32, shape, 1)


def picks(mask):
    return jnp.where(mask, 1.0, 0.0).astype(BF16)


def mm(a, b):
    return jnp.dot(a, b, preferred_element_type=F32)


def exact(a, b):
    return mm(a, b).astype(BF16)


def packed_shard(block):
    r, k = grid_of((256, 256))
    rows = picks(k == (r & 7) * 32 + ((r >> 3) & 1) * 16 + (r >> 4))
    return exact(rows, block.reshape(256, COLS)).reshape(16, 16, COLS)


def column_views(plane):
    l, k = grid_of((256, 384))
    return exact(plane.reshape(256, 256), picks(l == 2 * (k & 127) + (k >> 7) - 1))


def row_picker(offset_of, keep):
    row, k = grid_of((512, 256))
    h, r = row >> 4, row & 15
    hit = ((k >> 6) == (r & 3)) & ((k & 63) == 2 * h + offset_of(r)) & keep(r)
    return picks(hit)


def own_views(volume_ref, views_ref):
    picker = row_picker(lambda r: (r >> 2) - 1, lambda r: r < 12)
    for p in range(2):
        taken = exact(picker, column_views(volume_ref[:, p]))
        for s in range(2):
            for e in range(3):
                part = taken[256 * s : 256 * s + 256, 128 * e : 128 * e + 128]
                views_ref[:, s, 3 * p + e] = part.reshape(16, 16, COLS)


def halo_views(halo_ref, views_ref):
    columns = column_views(halo_ref[...])
    for b in range(2):
        taken = exact(row_picker(lambda r, b=b: b - 1, lambda r: r >= 12), columns)
        for s in range(2):
            for e in range(3):
                part = taken[256 * s : 256 * s + 256, 128 * e : 128 * e + 128]
                views_ref[:, s, 3 * b + e] += part.reshape(16, 16, COLS)
    last = jnp.zeros((512, COLS), F32)
    for e in range(3):
        picker = row_picker(lambda r: 1, lambda r, e=e: (r >> 2) == e)
        last = last + mm(picker, columns[:, 128 * e : 128 * e + 128])
    last = last.astype(BF16)
    for s in range(2):
        views_ref[:, s, 6] = last[256 * s : 256 * s + 256].reshape(16, 16, COLS)
        views_ref[:, s, 7] = jnp.zeros((16, 16, COLS), BF16)


def column_of(a, b, e):
    if a:
        return 16 * (3 * (a - 1) + e) + 4 * b
    return 16 * (3 * b + e) + 12 if b < 2 else 96 + 4 * e


def own_weights(weight_ref, chan):
    m, k = grid_of((144, 27 * 64))
    a, rest = m // 48, m % 48
    e, xy, slot, c = rest >> 4, (rest >> 3) & 1, (rest >> 2) & 1, rest & 3
    b = jnp.where(xy == 0, 1 + slot, 0)
    hit = (k == (9 * a + 3 * b + e) * 64 + CI * chan + c) & ((xy == 0) | (slot == 1))
    mine = exact(picks(hit), weight_ref[...].reshape(27 * 64, 128))
    o, k = grid_of((128, 256))
    spread = [exact(mine, picks((((k >> 3) & 1) == s) & (o == (k >> 4) * 8 + (k & 7)))) for s in range(2)]
    for_own = jnp.concatenate([spread[0][48:], spread[1][48:]], axis=0)
    for_next = jnp.concatenate([spread[0][:48], spread[1][:48]], axis=0)
    return for_own, for_next


def plane_of(ref):
    return jnp.concatenate([ref[:, hh].reshape(256, COLS) for hh in range(16)], axis=1)


def views_of(ref):
    return jnp.concatenate([ref[hh].reshape(256, COLS) for hh in range(16)], axis=1)


def kernel_terms(own_ref, views_ref):
    both = lax.dot_general(
        plane_of(own_ref), views_of(views_ref), (((1,), (1,)), ((), ())), preferred_element_type=F32
    ).reshape(16, 16, 256)
    return both[:, :8, :128] + both[:, 8:, 128:]


def input_terms(own_ref, next_ref, for_own, for_next):
    from_own = mm(for_own, plane_of(own_ref))
    from_next = mm(for_next, plane_of(next_ref))
    nothing = jnp.zeros((8, COLS), F32)
    w = lax.broadcasted_iota(jnp.int32, (8, 2048), 1) & 127

    def tap(product, tiles, tile, s):
        at = 16 * (s * tiles + tile)
        above = product[at + 8 : at + 16, COLS:]
        if s == 0:
            crossing = product[16 * tiles + 16 * tile + 8 : 16 * tiles + 16 * tile + 16, :COLS]
        else:
            crossing = nothing
        return product[at : at + 8] + jnp.concatenate([above, crossing], axis=1)

    r, k = grid_of((256, 256))
    lanes = picks(k == 2 * (r & 127) + (r >> 7))
    rows = picks(((r >> 6) == (k & 3)) & ((r & 63) == 2 * (k >> 3) + ((k >> 2) & 1)))
    planes = []
    for p in range(2):
        halves = []
        for s in range(2):
            by_e = [tap(from_own, 6, 3 * p + e, s) for e in range(3)]
            if p == 1:
                by_e = [by_e[e] + tap(from_next, 3, e, s) for e in range(3)]
            shifted = jnp.where(w == 127, 0.0, pltpu.roll(by_e[0], 2047, 1))
            even, odd = by_e[1], by_e[2] + shifted
            halves.append(
                jnp.concatenate(
                    [
                        jnp.concatenate([v[:, COLS * hh : COLS * hh + COLS] for hh in range(16)], axis=0)
                        for v in (even, odd)
                    ],
                    axis=1,
                )
            )
        mixed = jnp.concatenate(halves, axis=0).astype(BF16)
        planes.append(exact(rows, exact(mixed, lanes)).reshape(CI, 64, 256))
    return planes


def body(
    grad_ref, volume_hbm, weight_hbm, input_hbm, kernel_ref,
    own, nxt, views, volume, halo, weight, parts, arrived, result,
    recv_own, recv_next, recv_halo, recv_parts,
    send_x, send_z, send_chip, send_halo, send_parts, local, know,
):
    depth, chan = lax.axis_index("depth"), lax.axis_index("chan")
    core, zh, y = depth % 2, (depth // 2) % 4, depth // 8
    x, zl = chan % NX, chan // NX
    z = zh * NZL + zl

    def at(x_, y_, z_, core_):
        return ((y_ * 4 + z_ // NZL) * 2 + core_, (z_ % NZL) * NX + x_)

    xr, xl, x2 = (x + 1) % NX, (x + 3) % NX, (x + 2) % NX
    right, left = (depth, zl * NX + xr), (depth, zl * NX + xl)
    partner = (depth + 1 - 2 * core, chan)

    def up(n, core_=core):
        return at(x, y, (z + n) % NZ, core_), at(x, y, (z + NZ - n) % NZ, core_)

    beside = (at(x, (y + 1) % NY, z, core), at(x, (y + 3) % NY, z, core))

    take_volume = pltpu.make_async_copy(volume_hbm, volume, local.at[0])
    take_weight = pltpu.make_async_copy(weight_hbm, weight, local.at[1])
    take_volume.start()
    take_weight.start()

    barrier = pltpu.get_barrier_semaphore()
    for device in (right, left, *up(1), *up(1, 1 - core), *beside, partner):
        pl.semaphore_signal(barrier, inc=1, device_id=device, device_id_type=MESH)
    own[chan] = packed_shard(grad_ref[...].reshape(8, ROWS, COLS))
    pl.semaphore_wait(barrier, 9)

    def tell(devices, n):
        for device in devices:
            pl.semaphore_signal(know.at[n], inc=1, device_id=device, device_id_type=MESH)

    def hear(n):
        pl.semaphore_wait(know.at[n], 2)

    row = (zl, zl + 1 - 2 * (zl % 2), (zl + 2) % NZL, NZL - 1 - zl)
    column = tuple((depth, v * NX + x) for v in row)
    here = tuple(v * NX + x for v in row)
    from_left = tuple(v * NX + xl for v in row)
    from_right = tuple(v * NX + xr for v in row)
    across = tuple(v * NX + x2 for v in row)

    class Plane:
        def __init__(self, ref, recv, n):
            self.ref, self.recv, self.n = ref, recv, n

        def send(self, slot, device, sem):
            pltpu.make_async_remote_copy(
                self.ref.at[slot], self.ref.at[slot], sem, self.recv.at[slot],
                device_id=device, device_id_type=MESH,
            ).start()

        def to_right(self, slot):
            self.send(slot, right, send_x.at[self.n])

        def to_left(self, slot):
            self.send(slot, left, send_x.at[self.n])

        def to_sides(self, slot):
            self.to_right(slot)
            self.to_left(slot)

        def to_row(self, k):
            self.send(chan, column[k], send_z.at[self.n])

        def wait(self, slot):
            pltpu.make_async_remote_copy(
                self.ref.at[slot], self.ref.at[slot], send_x.at[self.n], self.recv.at[slot],
                device_id=partner, device_id_type=MESH,
            ).wait_recv()

        def sent(self):
            for sem, count in ((send_x, 12), (send_z, 3)):
                pltpu.make_async_remote_copy(
                    self.ref.at[pl.ds(0, count)], self.ref.at[pl.ds(0, count)], sem.at[self.n],
                    self.recv.at[0], device_id=partner, device_id_type=MESH,
                ).wait_send()

    mine, after = Plane(own, recv_own, 0), Plane(nxt, recv_next, 1)

    def to_partner(slot):
        return pltpu.make_async_remote_copy(
            own.at[slot], nxt.at[slot], send_chip, recv_next.at[slot],
            device_id=partner, device_id_type=MESH,
        )

    def hand(slot):
        @pl.when(core == 1)
        def _():
            to_partner(slot).start()

    def got(slot):
        mine.wait(slot)
        hand(slot)

    def plane_up():
        return pltpu.make_async_remote_copy(
            volume_hbm.at[:, 1], halo, send_halo.at[0], recv_halo,
            device_id=((depth + 1) % DEPTH, chan), device_id_type=MESH,
        )

    def shard_down():
        return pltpu.make_async_remote_copy(
            own.at[chan], nxt.at[chan], send_halo.at[1], recv_next.at[chan],
            device_id=((depth + DEPTH - 1) % DEPTH, chan), device_id_type=MESH,
        )

    mine.to_sides(chan)
    mine.to_row(1)
    hand(chan)

    @pl.when(core == 0)
    def _():
        plane_up().start()

    tell(up(1), 0)
    hear(0)
    mine.to_row(2)
    tell(up(2), 1)
    hear(1)
    mine.to_row(3)
    tell(beside, 2)
    hear(2)

    @pl.when((core == 0) & (depth > 0))
    def _():
        shard_down().start()

    @pl.when((core == 1) & (depth < DEPTH - 1))
    def _():
        plane_up().start()

    tell(up(4), 3)
    got(here[1])
    mine.to_sides(here[1])
    got(from_left[0])
    mine.to_right(from_left[0])
    got(from_right[0])
    take_volume.wait()
    own_views(volume, views)
    got(here[2])
    mine.to_sides(here[2])
    got(here[3])
    mine.to_sides(here[3])
    got(from_left[1])
    mine.to_right(from_left[1])
    got(from_right[1])
    got(from_left[2])
    got(from_right[2])
    mine.to_left(from_right[2])
    got(from_left[3])
    got(from_right[3])
    mine.to_left(from_right[3])
    hear(3)
    tell(beside, 4)

    gathers_next = (core == 1) & (depth < DEPTH - 1)

    @pl.when(gathers_next)
    def _():
        after.wait(chan)
        after.to_sides(chan)
        for k in range(1, 4):
            after.to_row(k)

    @pl.when(depth == DEPTH - 1)
    def _():
        nxt[...] = jnp.zeros_like(nxt)

    @pl.when(depth > 0)
    def _():
        plane_up().wait_recv()

    @pl.when(depth == 0)
    def _():
        halo[...] = jnp.zeros_like(halo)

    halo_views(halo, views)
    for k in range(4):
        got(across[k])
    hear(4)

    terms = kernel_terms(own, views)
    parts[:, 0] = terms[:, :4]
    parts[:, 1] = terms[:, 4:]

    def part_of(device):
        return parts.at[device // 2, device % 2]

    for n in range(1, DEPTH):
        peer = (depth + n) % DEPTH
        pltpu.make_async_remote_copy(
            part_of(peer), arrived.at[DEPTH - 1 - n], send_parts, recv_parts,
            device_id=(peer, chan), device_id_type=MESH,
        ).start()

    take_weight.wait()
    for_own, for_next = own_weights(weight, chan)

    @pl.when(gathers_next)
    def _():
        for k in range(1, 4):
            after.wait(here[k])
            after.to_sides(here[k])
        after.wait(from_left[0])
        after.to_right(from_left[0])
        after.wait(from_right[0])
        after.wait(from_left[1])
        after.to_right(from_left[1])
        after.wait(from_right[1])
        for k in range(2, 4):
            after.wait(from_left[k])
            after.wait(from_right[k])
            after.to_left(from_right[k])
        for k in range(4):
            after.wait(across[k])

    @pl.when(core == 0)
    def _():
        for slot in range(CHAN):
            after.wait(slot)

    planes = input_terms(own, nxt, for_own, for_next)
    for p in range(2):
        result[:, p] = planes[p]
    put = pltpu.make_async_copy(result, input_hbm, local.at[2])
    put.start()

    pltpu.make_async_remote_copy(
        arrived, arrived, send_parts, recv_parts, device_id=partner, device_id_type=MESH
    ).wait_recv()
    total = parts[depth // 2, depth % 2] + jnp.sum(arrived[...], axis=0)
    total = total * (1.0 / math.sqrt(DEPTH * ROWS * COLS))
    turned = jnp.transpose(jnp.concatenate([total, total], axis=0))
    for a in range(3):
        for b in range(3):
            for e in range(3):
                c = column_of(a, b, e)
                kernel_ref[9 * a + 3 * b + e] = turned[c : c + 4, :4]

    mine.sent()

    @pl.when(gathers_next)
    def _():
        after.sent()

    @pl.when(core == 1)
    def _():
        pltpu.make_async_remote_copy(
            own, nxt, send_chip, recv_next.at[0], device_id=partner, device_id_type=MESH
        ).wait_send()

    @pl.when(depth < DEPTH - 1)
    def _():
        plane_up().wait_send()

    @pl.when((core == 0) & (depth > 0))
    def _():
        shard_down().wait_send()

    pltpu.make_async_remote_copy(
        arrived, arrived, send_parts, recv_parts, device_id=partner, device_id_type=MESH
    ).wait_send()
    put.wait()


def shards(grad_out, volume, weight):
    any_space = pl.BlockSpec(memory_space=pl.ANY)
    in_vmem = pl.BlockSpec(memory_space=pltpu.VMEM)
    dma = pltpu.SemaphoreType.DMA
    plane = pltpu.VMEM((CHAN, 16, 16, COLS), BF16)
    return pl.pallas_call(
        body,
        out_shape=(
            jax.ShapeDtypeStruct(volume.shape, BF16),
            jax.ShapeDtypeStruct((27, CI, 4), F32),
        ),
        in_specs=[in_vmem, any_space, any_space],
        out_specs=(any_space, in_vmem),
        scratch_shapes=[
            plane,
            plane,
            pltpu.VMEM((16, 2, 8, 16, COLS), BF16),
            pltpu.VMEM(volume.shape, BF16),
            pltpu.VMEM((CI, 64, 256), BF16),
            pltpu.VMEM(weight.shape, BF16),
            pltpu.VMEM((16, 2, 4, 128), F32),
            pltpu.VMEM((DEPTH - 1, 4, 128), F32),
            pltpu.VMEM(volume.shape, BF16),
            dma((CHAN,)),
            dma((CHAN,)),
            dma,
            dma,
            dma((2,)),
            dma((2,)),
            dma,
            dma((2,)),
            dma,
            dma((3,)),
            pltpu.SemaphoreType.REGULAR((5,)),
        ],
        compiler_params=pltpu.CompilerParams(collective_id=0, has_side_effects=True),
    )(grad_out, volume, weight)


def solution(mesh):
    in_specs = (P("chan", "depth", None, None), P("chan", "depth", None, None), P())
    out_specs = (P("chan", "depth", None, None), P(None, "chan", "depth"))
    return jax.shard_map(shards, mesh=mesh, in_specs=in_specs, out_specs=out_specs, check_vma=False)
```

time: 411 us -> 46 us (0.11); the launches traced: 403 us -> 45.3 us
  blocking collectives: 171 us -> 0 us
  matrix products: 84 us -> 0 us
  waiting for transfers between devices: 62.8 us -> 0 us
  local copies, waits for them, and re-layouts: 53.7 us -> 3.17 us
  Pallas kernels: 0 us -> 41.5 us
  between operations: 14.9 us -> 0.64 us
  starting transfers between devices: 8.92 us -> 0 us
  other arithmetic: 7.28 us -> 0 us
    unnamed x1 -> x0, blocking collectives: 171 us -> none
    transpose x1 -> x0, matrix products: 83.3 us -> none  [weight_terms(): jnp.transpose(weight_cube, (2, 3, 4, 0, 1))]
    all_gather x1 -> x0, waiting for transfers between devices: 59.2 us -> none  [shards(): every_channel = lax.all_gather(grads_ext, 'chan', axis=0, tiled=True)]
    pallas_call x0 -> x1, Pallas kernels: none -> 41.5 us  [shards(): pl.pallas_call(body, out_shape=(jax.ShapeDtypeStruct(volume.shape, BF16),...]
    broadcast_in_dim x2 -> x0, local copies, waits for them, and re-layouts: 25.5 us -> none  [the longest x1 20.5 us: weight_terms(): inputs[None]]
    another operation x5 -> x0, local copies, waits for them, and re-layouts: 19.5 us -> none  [upsample(): paired = jnp.stack([even_cells, odd_cells], axis=coord_axis + 1)]
    ppermute x1 -> x0, starting transfers between devices: 8.88 us -> none  [from_behind(): return lax.ppermute(shard, axis, pairs)]
    another operation x6 -> x0, other arithmetic: 5.13 us -> none  [the longest x5 5.1 us: upsample(): paired = jnp.stack([even_cells, odd_cells], axis=coord_axis + 1)]
  transfers between devices with their start and end apart: 2 -> 0, of which waited for: 2 -> 0; matrix products, arithmetic and copies ran while one was open for 5% -> 0% of each run, Pallas kernels for 0% -> 0%
where the time goes in v1:
time: 46 us; the launch traced here: 45.3 us
  Pallas kernels  41.5 us (90%)
  local copies, waits for them, and re-layouts  3.17 us (7%)
  between operations  0.64 us (1%)
    pallas_call x1, Pallas kernels, shards(): pl.pallas_call(body, out_shape=(jax.ShapeDtypeStruct(volume.shape, BF16),...  41.5 us
    unnamed x1, local copies, waits for them, and re-layouts  1.67 us
    pallas_call x1, local copies, waits for them, and re-layouts, shards(): pl.pallas_call(body, out_shape=(jax.ShapeDtypeStruct(volume.shape, BF16),...  1.51 us

profile of v1, /device:TPU:1, one launch (start us, length us, event | category | flops | bytes accessed | tf_op | source)
XLA Modules:
  0.0 45.3 jit_solution(12494888709531626045)
XLA Ops:
  0.6 41.5 %shard_map.50 = (bf16[4,2,64,256]{3,2,1,0:T(8,128)(2,1)}, f32[27,4,4]{2,1,0:T(4,128)}) custom-call(bf16[8,1,32,128]{3,2,1,0:T(8,128)(2,1)} %grad_ref.1, bf16[4,2,64,256]{3,2,1,0:T(8,128)(2,1)} %volume_hbm.1, bf16[27,64,128]{2,1,0:T(8,128)(2,1)} %weight_hbm.1), custom_call_target="tpu_custom_call" | custom-call | tf_op jit(solution)/shard_map/pallas_call | solution.py:432
  42.1 1.5 %copy.5 = f32[27,4,4]{0,2,1:T(4,128)} copy(f32[27,4,4]{2,1,0:T(4,128)} %get-tuple-element.3) | data formatting | bytes 3456 | tf_op jit(solution)/shard_map/pallas_call | solution.py:432
  43.6 1.7 %copy.7 = bf16[4,2,64,256]{3,2,1,0:T(8,128)(2,1)} copy(bf16[4,2,64,256]{3,2,1,0:T(8,128)(2,1)} %get-tuple-element.6) | data formatting | bytes 524288

commit v2 on v1

--- a/solution.py
+++ b/solution.py
@@ -12,6 +12,7 @@
 F32 = jnp.float32
 NX, NY, NZ, NZL, DEPTH, CHAN = 4, 4, 16, 4, 32, 16
 CI, ROWS, COLS = 4, 32, 128
+FAR_FIRST = sorted(range(1, 32), key=lambda n: -(4 * min(n // 2 % 4, 4 - n // 2 % 4) + min(n // 8, 4 - n // 8)))
 
 
 def grid_of(shape):
@@ -153,8 +154,8 @@
 
 
 def body(
-    grad_ref, volume_hbm, weight_hbm, input_hbm, kernel_ref,
-    own, nxt, views, volume, halo, weight, parts, arrived, result,
+    grad_hbm, volume_hbm, weight_hbm, input_hbm, kernel_ref,
+    own, nxt, views, grad, volume, halo, weight, parts, arrived, result,
     recv_own, recv_next, recv_halo, recv_parts,
     send_x, send_z, send_chip, send_halo, send_parts, local, know,
 ):
@@ -162,6 +163,7 @@
     core, zh, y = depth % 2, (depth // 2) % 4, depth // 8
     x, zl = chan % NX, chan // NX
     z = zh * NZL + zl
+    middle = (zl == 1) | (zl == 2)
 
     def at(x_, y_, z_, core_):
         return ((y_ * 4 + z_ // NZL) * 2 + core_, (z_ % NZL) * NX + x_)
@@ -169,89 +171,123 @@
     xr, xl, x2 = (x + 1) % NX, (x + 3) % NX, (x + 2) % NX
     right, left = (depth, zl * NX + xr), (depth, zl * NX + xl)
     partner = (depth + 1 - 2 * core, chan)
-
-    def up(n, core_=core):
-        return at(x, y, (z + n) % NZ, core_), at(x, y, (z + NZ - n) % NZ, core_)
+    mate = (depth, (zl + 1 - 2 * (zl % 2)) * NX + x)
+    inner = (depth, (NZL - 1 - zl) * NX + x)
+
+    def up(n):
+        return at(x, y, (z + n) % NZ, core), at(x, y, (z + NZ - n) % NZ, core)
 
     beside = (at(x, (y + 1) % NY, z, core), at(x, (y + 3) % NY, z, core))
 
+    greets_up, greets_down = (zl == 3) & (zh < 3), z == 0
+    heard_down, heard_up = (zl == 0) & (zh > 0), z == NZ - 1
+    barrier = pltpu.get_barrier_semaphore()
+
+    def greet(device, sem=barrier):
+        pl.semaphore_signal(sem, inc=1, device_id=device, device_id_type=MESH)
+
+    def when(condition, act, *args):
+        pl.when(condition)(lambda: act(*args))
+
+    for device in (right, left, mate, partner):
+        greet(device)
+    when(middle, greet, inner)
+    when(greets_up, greet, up(1)[0])
+    when(greets_down, greet, up(1)[1])
+    when(y != 2, greet, at(x, y + 1 - 2 * (y // 3), z, core))
+    when(y == 0, greet, beside[1])
+
+    take_grad = pltpu.make_async_copy(grad_hbm, grad, local.at[3])
     take_volume = pltpu.make_async_copy(volume_hbm, volume, local.at[0])
     take_weight = pltpu.make_async_copy(weight_hbm, weight, local.at[1])
+    take_grad.start()
     take_volume.start()
     take_weight.start()
-
-    barrier = pltpu.get_barrier_semaphore()
-    for device in (right, left, *up(1), *up(1, 1 - core), *beside, partner):
-        pl.semaphore_signal(barrier, inc=1, device_id=device, device_id_type=MESH)
-    own[chan] = packed_shard(grad_ref[...].reshape(8, ROWS, COLS))
-    pl.semaphore_wait(barrier, 9)
-
-    def tell(devices, n):
-        for device in devices:
-            pl.semaphore_signal(know.at[n], inc=1, device_id=device, device_id_type=MESH)
-
-    def hear(n):
-        pl.semaphore_wait(know.at[n], 2)
-
-    row = (zl, zl + 1 - 2 * (zl % 2), (zl + 2) % NZL, NZL - 1 - zl)
-    column = tuple((depth, v * NX + x) for v in row)
+    take_grad.wait()
+    own[chan] = packed_shard(grad[...].reshape(8, ROWS, COLS))
+    greeted = 4 + jnp.where(middle, 1, 0) + jnp.where(heard_down | heard_up, 1, 0)
+    greeted = greeted + jnp.where(y == 2, 2, y % 2)
+    pl.semaphore_wait(barrier, greeted)
+
+    row = (zl, zl + 1 - 2 * (zl % 2), 2 - zl // 2, 3 - 3 * (zl // 2))
     here = tuple(v * NX + x for v in row)
     from_left = tuple(v * NX + xl for v in row)
     from_right = tuple(v * NX + xr for v in row)
     across = tuple(v * NX + x2 for v in row)
 
     class Plane:
-        def __init__(self, ref, recv, n):
-            self.ref, self.recv, self.n = ref, recv, n
-
-        def send(self, slot, device, sem):
+        def __init__(self, ref, recv, n, each):
+            self.ref, self.recv, self.n, self.each = ref, recv, n, each
+
+        def copy(self, slot, p, device, sem):
+            piece = self.ref.at[slot, pl.ds(8 * p, 8)]
+            return pltpu.make_async_remote_copy(
+                piece, piece, sem.at[self.n], self.recv.at[2 * slot + p],
+                device_id=device, device_id_type=MESH,
+            )
+
+        def send(self, slot, p, device, sem):
+            self.copy(slot, p, device, sem).start()
+
+        def sides(self, slot, p):
+            self.send(slot, p, right, send_x)
+            self.send(slot, p, left, send_x)
+
+        def wait(self, slot, p):
+            self.copy(slot, p, partner, send_x).wait_recv()
+
+        def begin(self):
+            for p in range(2):
+                self.sides(chan, p)
+                self.send(chan, p, mate, send_z)
+                when(middle, self.send, chan, p, inner, send_z)
+
+        def rows(self, k):
+            for p in range(2):
+                self.wait(here[k], p)
+                self.sides(here[k], p)
+                when(middle, self.send, here[k], p, inner if k == 1 else mate, send_z)
+            self.each(here[k])
+
+        def turns(self, k):
+            for p in range(2):
+                self.wait(from_left[k], p)
+                if p == 0:
+                    self.send(from_left[k], p, right, send_x)
+                self.wait(from_right[k], p)
+                if p == 1:
+                    self.send(from_right[k], p, left, send_x)
+            self.each(from_left[k])
+            self.each(from_right[k])
+
+        def ends(self):
+            for k in range(4):
+                for p in range(2):
+                    self.wait(across[k], p)
+                self.each(across[k])
+
+        def drained(self, sem, count):
+            shards_ = self.ref.at[pl.ds(0, count)]
             pltpu.make_async_remote_copy(
-                self.ref.at[slot], self.ref.at[slot], sem, self.recv.at[slot],
-                device_id=device, device_id_type=MESH,
-            ).start()
-
-        def to_right(self, slot):
-            self.send(slot, right, send_x.at[self.n])
-
-        def to_left(self, slot):
-            self.send(slot, left, send_x.at[self.n])
-
-        def to_sides(self, slot):
-            self.to_right(slot)
-            self.to_left(slot)
-
-        def to_row(self, k):
-            self.send(chan, column[k], send_z.at[self.n])
-
-        def wait(self, slot):
-            pltpu.make_async_remote_copy(
-                self.ref.at[slot], self.ref.at[slot], send_x.at[self.n], self.recv.at[slot],
-                device_id=partner, device_id_type=MESH,
-            ).wait_recv()
+                shards_, shards_, sem.at[self.n], self.recv.at[0], device_id=partner, device_id_type=MESH
+            ).wait_send()
 
         def sent(self):
-            for sem, count in ((send_x, 12), (send_z, 3)):
-                pltpu.make_async_remote_copy(
-                    self.ref.at[pl.ds(0, count)], self.ref.at[pl.ds(0, count)], sem.at[self.n],
-                    self.recv.at[0], device_id=partner, device_id_type=MESH,
-                ).wait_send()
-
-    mine, after = Plane(own, recv_own, 0), Plane(nxt, recv_next, 1)
+            self.drained(send_x, 12)
+            when(middle, self.drained, send_z, 5)
+            when(jnp.logical_not(middle), self.drained, send_z, 1)
 
     def to_partner(slot):
         return pltpu.make_async_remote_copy(
-            own.at[slot], nxt.at[slot], send_chip, recv_next.at[slot],
+            own.at[slot], nxt.at[slot], send_chip, recv_next.at[2 * slot],
             device_id=partner, device_id_type=MESH,
         )
 
     def hand(slot):
-        @pl.when(core == 1)
-        def _():
-            to_partner(slot).start()
-
-    def got(slot):
-        mine.wait(slot)
-        hand(slot)
+        when(core == 1, lambda: to_partner(slot).start())
+
+    mine = Plane(own, recv_own, 0, hand)
+    after = Plane(nxt, recv_next, 1, lambda slot: None)
 
     def plane_up():
         return pltpu.make_async_remote_copy(
@@ -261,134 +297,127 @@
 
     def shard_down():
         return pltpu.make_async_remote_copy(
-            own.at[chan], nxt.at[chan], send_halo.at[1], recv_next.at[chan],
+            own.at[chan], nxt.at[chan], send_halo.at[1], recv_next.at[2 * chan],
             device_id=((depth + DEPTH - 1) % DEPTH, chan), device_id_type=MESH,
         )
 
-    mine.to_sides(chan)
-    mine.to_row(1)
+    def tell(n, *devices):
+        for device in devices:
+            greet(device, know.at[n])
+
+    def hear(n, count=2):
+        pl.semaphore_wait(know.at[n], count)
+
+    def neighbours():
+        when(greets_up | greets_down, hear, 0, 1)
+        when(y == 0, hear, 7, 2)
+        when(y % 2 == 1, hear, 7, 1)
+        tell(1, *up(1))
+
+    def two_away():
+        hear(1)
+        tell(2, *up(2))
+
+    def four_away():
+        hear(2)
+        tell(3, partner)
+        hear(3, 1)
+        when((core == 1) & (zh < 3), lambda: plane_up().start())
+        when((core == 0) & (zh > 0), lambda: shard_down().start())
+        tell(4, *beside)
+
+    def next_row():
+        hear(4)
+        when((core == 1) & (zh == 3) & (y < NY - 1), lambda: plane_up().start())
+        when((core == 0) & (zh == 0) & (y > 0), lambda: shard_down().start())
+        tell(5, *up(4))
+
+    def all_rows():
+        hear(5)
+        tell(6, *beside)
+
+    late = zh > 0
+    early = zh == 0
+    mine.begin()
     hand(chan)
-
-    @pl.when(core == 0)
-    def _():
-        plane_up().start()
-
-    tell(up(1), 0)
-    hear(0)
-    mine.to_row(2)
-    tell(up(2), 1)
-    hear(1)
-    mine.to_row(3)
-    tell(beside, 2)
-    hear(2)
-
-    @pl.when((core == 0) & (depth > 0))
-    def _():
-        shard_down().start()
-
-    @pl.when((core == 1) & (depth < DEPTH - 1))
-    def _():
-        plane_up().start()
-
-    tell(up(4), 3)
-    got(here[1])
-    mine.to_sides(here[1])
-    got(from_left[0])
-    mine.to_right(from_left[0])
-    got(from_right[0])
+    when(core == 0, lambda: plane_up().start())
+    when(heard_down, tell, 0, up(1)[1])
+    when(heard_up, tell, 0, up(1)[0])
+    when(y % 2 == 1, tell, 7, at(x, 0, z, core))
+    when(y == 2, tell, 7, *beside)
+    mine.rows(1)
+    when(late, neighbours)
+    mine.turns(0)
+    when(late, two_away)
     take_volume.wait()
     own_views(volume, views)
-    got(here[2])
-    mine.to_sides(here[2])
-    got(here[3])
-    mine.to_sides(here[3])
-    got(from_left[1])
-    mine.to_right(from_left[1])
-    got(from_right[1])
-    got(from_left[2])
-    got(from_right[2])
-    mine.to_left(from_right[2])
-    got(from_left[3])
-    got(from_right[3])
-    mine.to_left(from_right[3])
-    hear(3)
-    tell(beside, 4)
-
+    mine.rows(2)
+    when(late, four_away)
+    mine.rows(3)
+    mine.turns(1)
+    when(late, next_row)
+    mine.turns(2)
+    when(early, neighbours)
+    mine.turns(3)
+    when(early, two_away)
+    when(late, all_rows)
+    when(early, four_away)
+    mine.ends()
+    when(early, next_row)
+    when(depth > 0, lambda: plane_up().wait_recv())
+
+    @pl.when(depth == 0)
+    def _():
+        halo[...] = jnp.zeros_like(halo)
+
+    halo_views(halo, views)
+    terms = kernel_terms(own, views)
+    parts[:, 0] = terms[:, :4]
+    parts[:, 1] = terms[:, 4:]
+    when(early, all_rows)
+    hear(6)
+    for step in FAR_FIRST:
+        dy, dz, dc = step // 8, (step // 2) % 4, step % 2
+        peer = (((y + dy) % NY) * 4 + (zh + dz) % 4) * 2 + (core + dc) % 2
+        pltpu.make_async_remote_copy(
+            parts.at[peer // 2, peer % 2], arrived.at[step - 1], send_parts, recv_parts,
+            device_id=(peer, chan), device_id_type=MESH,
+        ).start()
+
+    take_weight.wait()
+    for_own, for_next = own_weights(weight, chan)
     gathers_next = (core == 1) & (depth < DEPTH - 1)
 
     @pl.when(gathers_next)
     def _():
-        after.wait(chan)
-        after.to_sides(chan)
+        shard_down().wait_recv()
+        after.begin()
+        after.rows(1)
+        after.turns(0)
+        after.rows(2)
+        after.rows(3)
         for k in range(1, 4):
-            after.to_row(k)
+            after.turns(k)
+        after.ends()
 
     @pl.when(depth == DEPTH - 1)
     def _():
         nxt[...] = jnp.zeros_like(nxt)
 
-    @pl.when(depth > 0)
-    def _():
-        plane_up().wait_recv()
-
-    @pl.when(depth == 0)
-    def _():
-        halo[...] = jnp.zeros_like(halo)
-
-    halo_views(halo, views)
-    for k in range(4):
-        got(across[k])
-    hear(4)
-
-    terms = kernel_terms(own, views)
-    parts[:, 0] = terms[:, :4]
-    parts[:, 1] = terms[:, 4:]
-
-    def part_of(device):
-        return parts.at[device // 2, device % 2]
-
-    for n in range(1, DEPTH):
-        peer = (depth + n) % DEPTH
-        pltpu.make_async_remote_copy(
-            part_of(peer), arrived.at[DEPTH - 1 - n], send_parts, recv_parts,
-            device_id=(peer, chan), device_id_type=MESH,
-        ).start()
-
-    take_weight.wait()
-    for_own, for_next = own_weights(weight, chan)
-
-    @pl.when(gathers_next)
-    def _():
-        for k in range(1, 4):
-            after.wait(here[k])
-            after.to_sides(here[k])
-        after.wait(from_left[0])
-        after.to_right(from_left[0])
-        after.wait(from_right[0])
-        after.wait(from_left[1])
-        after.to_right(from_left[1])
-        after.wait(from_right[1])
-        for k in range(2, 4):
-            after.wait(from_left[k])
-            after.wait(from_right[k])
-            after.to_left(from_right[k])
-        for k in range(4):
-            after.wait(across[k])
-
     @pl.when(core == 0)
     def _():
         for slot in range(CHAN):
-            after.wait(slot)
+            to_partner(slot).wait_recv()
 
     planes = input_terms(own, nxt, for_own, for_next)
     for p in range(2):
         result[:, p] = planes[p]
     put = pltpu.make_async_copy(result, input_hbm, local.at[2])
     put.start()
-
-    pltpu.make_async_remote_copy(
+    every_part = pltpu.make_async_remote_copy(
         arrived, arrived, send_parts, recv_parts, device_id=partner, device_id_type=MESH
-    ).wait_recv()
+    )
+    every_part.wait_recv()
     total = parts[depth // 2, depth % 2] + jnp.sum(arrived[...], axis=0)
     total = total * (1.0 / math.sqrt(DEPTH * ROWS * COLS))
     turned = jnp.transpose(jnp.concatenate([total, total], axis=0))
@@ -397,12 +426,8 @@
             for e in range(3):
                 c = column_of(a, b, e)
                 kernel_ref[9 * a + 3 * b + e] = turned[c : c + 4, :4]
-
     mine.sent()
-
-    @pl.when(gathers_next)
-    def _():
-        after.sent()
+    when(gathers_next, after.sent)
 
     @pl.when(core == 1)
     def _():
@@ -410,17 +435,9 @@
             own, nxt, send_chip, recv_next.at[0], device_id=partner, device_id_type=MESH
         ).wait_send()
 
-    @pl.when(depth < DEPTH - 1)
-    def _():
-        plane_up().wait_send()
-
-    @pl.when((core == 0) & (depth > 0))
-    def _():
-        shard_down().wait_send()
-
-    pltpu.make_async_remote_copy(
-        arrived, arrived, send_parts, recv_parts, device_id=partner, device_id_type=MESH
-    ).wait_send()
+    when(depth < DEPTH - 1, lambda: plane_up().wait_send())
+    when((core == 0) & (depth > 0), lambda: shard_down().wait_send())
+    every_part.wait_send()
     put.wait()
 
 
@@ -435,20 +452,21 @@
             jax.ShapeDtypeStruct(volume.shape, BF16),
             jax.ShapeDtypeStruct((27, CI, 4), F32),
         ),
-        in_specs=[in_vmem, any_space, any_space],
+        in_specs=[any_space, any_space, any_space],
         out_specs=(any_space, in_vmem),
         scratch_shapes=[
             plane,
             plane,
             pltpu.VMEM((16, 2, 8, 16, COLS), BF16),
+            pltpu.VMEM(grad_out.shape, BF16),
             pltpu.VMEM(volume.shape, BF16),
             pltpu.VMEM((CI, 64, 256), BF16),
             pltpu.VMEM(weight.shape, BF16),
             pltpu.VMEM((16, 2, 4, 128), F32),
             pltpu.VMEM((DEPTH - 1, 4, 128), F32),
             pltpu.VMEM(volume.shape, BF16),
-            dma((CHAN,)),
-            dma((CHAN,)),
+            dma((2 * CHAN,)),
+            dma((2 * CHAN,)),
             dma,
             dma,
             dma((2,)),
@@ -456,8 +474,8 @@
             dma,
             dma((2,)),
             dma,
-            dma((3,)),
-            pltpu.SemaphoreType.REGULAR((5,)),
+            dma((4,)),
+            pltpu.SemaphoreType.REGULAR((8,)),
         ],
         compiler_params=pltpu.CompilerParams(collective_id=0, has_side_effects=True),
     )(grad_out, volume, weight)

time: 46 us -> 55.3 us (1.20); the launches traced: 45.3 us -> 55.1 us
  Pallas kernels: 41.5 us -> 51.3 us
    pallas_call x1, Pallas kernels: 41.5 us -> 51.3 us  [shards(): pl.pallas_call(body, out_shape=(jax.ShapeDtypeStruct(volume.shape, BF16),...]
where the time goes in v2:
time: 55.3 us; the launch traced here: 55.1 us
  Pallas kernels  51.3 us (93%)
  local copies, waits for them, and re-layouts  3.17 us (6%)
  between operations  0.64 us (1%)
    pallas_call x1, Pallas kernels, shards(): pl.pallas_call(body, out_shape=(jax.ShapeDtypeStruct(volume.shape, BF16),...  51.3 us
    unnamed x1, local copies, waits for them, and re-layouts  1.67 us
    pallas_call x1, local copies, waits for them, and re-layouts, shards(): pl.pallas_call(body, out_shape=(jax.ShapeDtypeStruct(volume.shape, BF16),...  1.51 us

profile of v2, /device:TPU:1, one launch (start us, length us, event | category | flops | bytes accessed | tf_op | source)
XLA Modules:
  0.0 55.1 jit_solution(3407598339716039509)
XLA Ops:
  0.6 51.3 %shard_map.50 = (bf16[4,2,64,256]{3,2,1,0:T(8,128)(2,1)}, f32[27,4,4]{2,1,0:T(4,128)}) custom-call(bf16[8,1,32,128]{3,2,1,0:T(8,128)(2,1)} %grad_hbm.1, bf16[4,2,64,256]{3,2,1,0:T(8,128)(2,1)} %volume_hbm.1, bf16[27,64,128]{2,1,0:T(8,128)(2,1)} %weight_hbm.1), custom_call_target="tpu_custom_call" | custom-call | tf_op jit(solution)/shard_map/pallas_call | solution.py:449
  52.0 1.5 %copy.5 = f32[27,4,4]{0,2,1:T(4,128)} copy(f32[27,4,4]{2,1,0:T(4,128)} %get-tuple-element.3) | data formatting | bytes 3456 | tf_op jit(solution)/shard_map/pallas_call | solution.py:449
  53.5 1.7 %copy.7 = bf16[4,2,64,256]{3,2,1,0:T(8,128)(2,1)} copy(bf16[4,2,64,256]{3,2,1,0:T(8,128)(2,1)} %get-tuple-element.6) | data formatting | bytes 524288

commit v3 on v2

--- a/solution.py
+++ b/solution.py
@@ -163,7 +163,6 @@
     core, zh, y = depth % 2, (depth // 2) % 4, depth // 8
     x, zl = chan % NX, chan // NX
     z = zh * NZL + zl
-    middle = (zl == 1) | (zl == 2)
 
     def at(x_, y_, z_, core_):
         return ((y_ * 4 + z_ // NZL) * 2 + core_, (z_ % NZL) * NX + x_)
@@ -171,100 +170,72 @@
     xr, xl, x2 = (x + 1) % NX, (x + 3) % NX, (x + 2) % NX
     right, left = (depth, zl * NX + xr), (depth, zl * NX + xl)
     partner = (depth + 1 - 2 * core, chan)
-    mate = (depth, (zl + 1 - 2 * (zl % 2)) * NX + x)
-    inner = (depth, (NZL - 1 - zl) * NX + x)
+    far = (depth, zl * NX + x2)
+    row = (zl, zl + 1 - 2 * (zl % 2), (zl + 2) % NZL, NZL - 1 - zl)
+    column = tuple((depth, v * NX + x) for v in row)
+    here = tuple(v * NX + x for v in row)
+    others = tuple(tuple(v * NX + c for c in (xl, xr, x2)) for v in row)
 
     def up(n):
         return at(x, y, (z + n) % NZ, core), at(x, y, (z + NZ - n) % NZ, core)
 
     beside = (at(x, (y + 1) % NY, z, core), at(x, (y + 3) % NY, z, core))
 
+    barrier = pltpu.get_barrier_semaphore()
+
+    def greet(device, sem=barrier):
+        pl.semaphore_signal(sem, inc=1, device_id=device, device_id_type=MESH)
+
+    def when(condition, act, *args):
+        pl.when(condition)(lambda: act(*args))
+
+    for device in (far, right, left, *column[1:], partner):
+        greet(device)
+    take_grad = pltpu.make_async_copy(grad_hbm, grad, local.at[3])
+    take_grad.start()
+    above, below = ((depth + 1) % DEPTH, chan), ((depth + DEPTH - 1) % DEPTH, chan)
+    has_above, has_below = depth < DEPTH - 1, depth > 0
+    calls_above, calls_below = (core == 1) & (zh < 3), (core == 0) & (zh == 0) & has_below
+    heard_below, heard_above = (core == 0) & (zh > 0), (core == 1) & (zh == 3) & has_above
     greets_up, greets_down = (zl == 3) & (zh < 3), z == 0
     heard_down, heard_up = (zl == 0) & (zh > 0), z == NZ - 1
-    barrier = pltpu.get_barrier_semaphore()
-
-    def greet(device, sem=barrier):
-        pl.semaphore_signal(sem, inc=1, device_id=device, device_id_type=MESH)
-
-    def when(condition, act, *args):
-        pl.when(condition)(lambda: act(*args))
-
-    for device in (right, left, mate, partner):
-        greet(device)
-    when(middle, greet, inner)
+    when(calls_above, greet, above)
+    when(calls_below, greet, below)
     when(greets_up, greet, up(1)[0])
     when(greets_down, greet, up(1)[1])
     when(y != 2, greet, at(x, y + 1 - 2 * (y // 3), z, core))
     when(y == 0, greet, beside[1])
-
-    take_grad = pltpu.make_async_copy(grad_hbm, grad, local.at[3])
     take_volume = pltpu.make_async_copy(volume_hbm, volume, local.at[0])
     take_weight = pltpu.make_async_copy(weight_hbm, weight, local.at[1])
-    take_grad.start()
     take_volume.start()
     take_weight.start()
     take_grad.wait()
     own[chan] = packed_shard(grad[...].reshape(8, ROWS, COLS))
-    greeted = 4 + jnp.where(middle, 1, 0) + jnp.where(heard_down | heard_up, 1, 0)
-    greeted = greeted + jnp.where(y == 2, 2, y % 2)
+    greeted = 7 + jnp.where(heard_down | heard_up, 1, 0)
+    greeted = greeted + jnp.where(y == 2, 2, y % 2) + jnp.where(heard_below | heard_above, 1, 0)
     pl.semaphore_wait(barrier, greeted)
 
-    row = (zl, zl + 1 - 2 * (zl % 2), 2 - zl // 2, 3 - 3 * (zl // 2))
-    here = tuple(v * NX + x for v in row)
-    from_left = tuple(v * NX + xl for v in row)
-    from_right = tuple(v * NX + xr for v in row)
-    across = tuple(v * NX + x2 for v in row)
-
     class Plane:
-        def __init__(self, ref, recv, n, each):
-            self.ref, self.recv, self.n, self.each = ref, recv, n, each
-
-        def copy(self, slot, p, device, sem):
-            piece = self.ref.at[slot, pl.ds(8 * p, 8)]
+        def __init__(self, ref, recv, n):
+            self.ref, self.recv, self.n = ref, recv, n
+
+        def copy(self, slot, device, sem):
             return pltpu.make_async_remote_copy(
-                piece, piece, sem.at[self.n], self.recv.at[2 * slot + p],
+                self.ref.at[slot], self.ref.at[slot], sem.at[self.n], self.recv.at[slot],
                 device_id=device, device_id_type=MESH,
             )
 
-        def send(self, slot, p, device, sem):
-            self.copy(slot, p, device, sem).start()
-
-        def sides(self, slot, p):
-            self.send(slot, p, right, send_x)
-            self.send(slot, p, left, send_x)
-
-        def wait(self, slot, p):
-            self.copy(slot, p, partner, send_x).wait_recv()
+        def sides(self, slot):
+            for device in (far, right, left):
+                self.copy(slot, device, send_x).start()
 
         def begin(self):
-            for p in range(2):
-                self.sides(chan, p)
-                self.send(chan, p, mate, send_z)
-                when(middle, self.send, chan, p, inner, send_z)
-
-        def rows(self, k):
-            for p in range(2):
-                self.wait(here[k], p)
-                self.sides(here[k], p)
-                when(middle, self.send, here[k], p, inner if k == 1 else mate, send_z)
-            self.each(here[k])
-
-        def turns(self, k):
-            for p in range(2):
-                self.wait(from_left[k], p)
-                if p == 0:
-                    self.send(from_left[k], p, right, send_x)
-                self.wait(from_right[k], p)
-                if p == 1:
-                    self.send(from_right[k], p, left, send_x)
-            self.each(from_left[k])
-            self.each(from_right[k])
-
-        def ends(self):
-            for k in range(4):
-                for p in range(2):
-                    self.wait(across[k], p)
-                self.each(across[k])
+            self.sides(chan)
+            for k in range(1, 4):
+                self.copy(chan, column[k], send_z).start()
+
+        def wait(self, slot):
+            self.copy(slot, partner, send_x).wait_recv()
 
         def drained(self, sem, count):
             shards_ = self.ref.at[pl.ds(0, count)]
@@ -274,20 +245,28 @@
 
         def sent(self):
             self.drained(send_x, 12)
-            when(middle, self.drained, send_z, 5)
-            when(jnp.logical_not(middle), self.drained, send_z, 1)
+            self.drained(send_z, 3)
 
     def to_partner(slot):
         return pltpu.make_async_remote_copy(
-            own.at[slot], nxt.at[slot], send_chip, recv_next.at[2 * slot],
+            own.at[slot], nxt.at[slot], send_chip, recv_next.at[slot],
             device_id=partner, device_id_type=MESH,
         )
 
     def hand(slot):
         when(core == 1, lambda: to_partner(slot).start())
 
-    mine = Plane(own, recv_own, 0, hand)
-    after = Plane(nxt, recv_next, 1, lambda slot: None)
+    mine, after = Plane(own, recv_own, 0), Plane(nxt, recv_next, 1)
+
+    def row_at(k):
+        mine.wait(here[k])
+        mine.sides(here[k])
+        hand(here[k])
+
+    def rest_of(k):
+        for slot in others[k]:
+            mine.wait(slot)
+            hand(slot)
 
     def plane_up():
         return pltpu.make_async_remote_copy(
@@ -297,7 +276,7 @@
 
     def shard_down():
         return pltpu.make_async_remote_copy(
-            own.at[chan], nxt.at[chan], send_halo.at[1], recv_next.at[2 * chan],
+            own.at[chan], nxt.at[chan], send_halo.at[1], recv_next.at[chan],
             device_id=((depth + DEPTH - 1) % DEPTH, chan), device_id_type=MESH,
         )
 
@@ -322,59 +301,73 @@
         hear(2)
         tell(3, partner)
         hear(3, 1)
-        when((core == 1) & (zh < 3), lambda: plane_up().start())
-        when((core == 0) & (zh > 0), lambda: shard_down().start())
         tell(4, *beside)
 
     def next_row():
         hear(4)
-        when((core == 1) & (zh == 3) & (y < NY - 1), lambda: plane_up().start())
-        when((core == 0) & (zh == 0) & (y > 0), lambda: shard_down().start())
         tell(5, *up(4))
 
     def all_rows():
         hear(5)
         tell(6, *beside)
 
-    late = zh > 0
-    early = zh == 0
+    def trade_down():
+        hear(8, 1)
+        shard_down().start()
+
+    def trade_up():
+        hear(8, 1)
+        plane_up().start()
+
+    def next_rows():
+        shard_down().wait_recv()
+        after.begin()
+        for k in range(1, 4):
+            after.wait(here[k])
+            after.sides(here[k])
+
+    late, early = zh > 0, zh == 0
+    gathers_next = (core == 1) & has_above
     mine.begin()
     hand(chan)
     when(core == 0, lambda: plane_up().start())
+    when(heard_below, tell, 8, below)
+    when(heard_above, tell, 8, above)
     when(heard_down, tell, 0, up(1)[1])
     when(heard_up, tell, 0, up(1)[0])
     when(y % 2 == 1, tell, 7, at(x, 0, z, core))
     when(y == 2, tell, 7, *beside)
-    mine.rows(1)
+    when(heard_below, lambda: shard_down().start())
+    row_at(1)
     when(late, neighbours)
-    mine.turns(0)
+    row_at(2)
     when(late, two_away)
+    row_at(3)
+    when(early, neighbours)
     take_volume.wait()
     own_views(volume, views)
-    mine.rows(2)
-    when(late, four_away)
-    mine.rows(3)
-    mine.turns(1)
-    when(late, next_row)
-    mine.turns(2)
-    when(early, neighbours)
-    mine.turns(3)
+    when(heard_above, lambda: plane_up().start())
+    when(calls_above, trade_up)
     when(early, two_away)
-    when(late, all_rows)
-    when(early, four_away)
-    mine.ends()
-    when(early, next_row)
-    when(depth > 0, lambda: plane_up().wait_recv())
+    four_away()
+    when(calls_below, trade_down)
+    rest_of(0)
+    next_row()
+    rest_of(1)
+    when(has_below, lambda: plane_up().wait_recv())
 
     @pl.when(depth == 0)
     def _():
         halo[...] = jnp.zeros_like(halo)
 
     halo_views(halo, views)
+    when(gathers_next & (zh < 2), next_rows)
+    rest_of(2)
+    all_rows()
+    rest_of(3)
     terms = kernel_terms(own, views)
     parts[:, 0] = terms[:, :4]
     parts[:, 1] = terms[:, 4:]
-    when(early, all_rows)
     hear(6)
     for step in FAR_FIRST:
         dy, dz, dc = step // 8, (step // 2) % 4, step % 2
@@ -386,19 +379,13 @@
 
     take_weight.wait()
     for_own, for_next = own_weights(weight, chan)
-    gathers_next = (core == 1) & (depth < DEPTH - 1)
+    when(gathers_next & (zh >= 2), next_rows)
 
     @pl.when(gathers_next)
     def _():
-        shard_down().wait_recv()
-        after.begin()
-        after.rows(1)
-        after.turns(0)
-        after.rows(2)
-        after.rows(3)
-        for k in range(1, 4):
-            after.turns(k)
-        after.ends()
+        for k in range(4):
+            for slot in others[k]:
+                after.wait(slot)
 
     @pl.when(depth == DEPTH - 1)
     def _():
@@ -465,8 +452,8 @@
             pltpu.VMEM((16, 2, 4, 128), F32),
             pltpu.VMEM((DEPTH - 1, 4, 128), F32),
             pltpu.VMEM(volume.shape, BF16),
-            dma((2 * CHAN,)),
-            dma((2 * CHAN,)),
+            dma((CHAN,)),
+            dma((CHAN,)),
             dma,
             dma,
             dma((2,)),
@@ -475,7 +462,7 @@
             dma((2,)),
             dma,
             dma((4,)),
-            pltpu.SemaphoreType.REGULAR((8,)),
+            pltpu.SemaphoreType.REGULAR((9,)),
         ],
         compiler_params=pltpu.CompilerParams(collective_id=0, has_side_effects=True),
     )(grad_out, volume, weight)

time: 55.3 us -> 44 us (0.80)
  Pallas kernels: 51.3 us -> 40 us
    pallas_call x1, Pallas kernels: 51.3 us -> 40 us  [shards(): pl.pallas_call(body, out_shape=(jax.ShapeDtypeStruct(volume.shape, BF16),...]
where the time goes in v3:
time: 44 us; the launch traced here: 43.8 us
  Pallas kernels  40 us (91%)
  local copies, waits for them, and re-layouts  3.17 us (7%)
  between operations  0.64 us (1%)
    pallas_call x1, Pallas kernels, shards(): pl.pallas_call(body, out_shape=(jax.ShapeDtypeStruct(volume.shape, BF16),...  40 us
    unnamed x1, local copies, waits for them, and re-layouts  1.67 us
    pallas_call x1, local copies, waits for them, and re-layouts, shards(): pl.pallas_call(body, out_shape=(jax.ShapeDtypeStruct(volume.shape, BF16),...  1.51 us

profile of v3, /device:TPU:1, one launch (start us, length us, event | category | flops | bytes accessed | tf_op | source)
XLA Modules:
  0.0 43.8 jit_solution(13654974449523527215)
XLA Ops:
  0.6 40.0 %shard_map.50 = (bf16[4,2,64,256]{3,2,1,0:T(8,128)(2,1)}, f32[27,4,4]{2,1,0:T(4,128)}) custom-call(bf16[8,1,32,128]{3,2,1,0:T(8,128)(2,1)} %grad_hbm.1, bf16[4,2,64,256]{3,2,1,0:T(8,128)(2,1)} %volume_hbm.1, bf16[27,64,128]{2,1,0:T(8,128)(2,1)} %weight_hbm.1), custom_call_target="tpu_custom_call" | custom-call | tf_op jit(solution)/shard_map/pallas_call | solution.py:436
  40.7 1.5 %copy.5 = f32[27,4,4]{0,2,1:T(4,128)} copy(f32[27,4,4]{2,1,0:T(4,128)} %get-tuple-element.3) | data formatting | bytes 3456 | tf_op jit(solution)/shard_map/pallas_call | solution.py:436
  42.2 1.7 %copy.7 = bf16[4,2,64,256]{3,2,1,0:T(8,128)(2,1)} copy(bf16[4,2,64,256]{3,2,1,0:T(8,128)(2,1)} %get-tuple-element.6) | data formatting | bytes 524288

commit v4 on v3

--- a/solution.py
+++ b/solution.py
@@ -77,10 +77,12 @@
         views_ref[:, s, 7] = jnp.zeros((16, 16, COLS), BF16)
 
 
-def column_of(a, b, e):
-    if a:
-        return 16 * (3 * (a - 1) + e) + 4 * b
-    return 16 * (3 * b + e) + 12 if b < 2 else 96 + 4 * e
+def column_order():
+    col, k = grid_of((128, 128))
+    c, t = k >> 5, k & 31
+    a, b, e = t // 9, (t // 3) % 3, t % 3
+    source = jnp.where(a > 0, 16 * (3 * a - 3 + e) + 4 * b, jnp.where(b < 2, 16 * (3 * b + e) + 12, 96 + 4 * e))
+    return jnp.where((col == source + c) & (t < 27), 1.0, 0.0)
 
 
 def own_weights(weight_ref, chan):
@@ -154,8 +156,8 @@
 
 
 def body(
-    grad_hbm, volume_hbm, weight_hbm, input_hbm, kernel_ref,
-    own, nxt, views, grad, volume, halo, weight, parts, arrived, result,
+    grad_hbm, volume_hbm, weight_hbm, result, kernel_ref,
+    own, nxt, views, grad, volume, halo, weight, parts, arrived,
     recv_own, recv_next, recv_halo, recv_parts,
     send_x, send_z, send_chip, send_halo, send_parts, local, know,
 ):
@@ -399,20 +401,18 @@
     planes = input_terms(own, nxt, for_own, for_next)
     for p in range(2):
         result[:, p] = planes[p]
-    put = pltpu.make_async_copy(result, input_hbm, local.at[2])
-    put.start()
+    choose = column_order()
     every_part = pltpu.make_async_remote_copy(
         arrived, arrived, send_parts, recv_parts, device_id=partner, device_id_type=MESH
     )
     every_part.wait_recv()
     total = parts[depth // 2, depth % 2] + jnp.sum(arrived[...], axis=0)
-    total = total * (1.0 / math.sqrt(DEPTH * ROWS * COLS))
-    turned = jnp.transpose(jnp.concatenate([total, total], axis=0))
-    for a in range(3):
-        for b in range(3):
-            for e in range(3):
-                c = column_of(a, b, e)
-                kernel_ref[9 * a + 3 * b + e] = turned[c : c + 4, :4]
+    chosen = jnp.dot(
+        jnp.concatenate([total, total], axis=0), choose, precision=lax.Precision.HIGHEST, preferred_element_type=F32
+    )
+    chosen = chosen * (1.0 / math.sqrt(DEPTH * ROWS * COLS))
+    for c in range(CI):
+        kernel_ref[c] = chosen[:4, 32 * c : 32 * c + 27]
     mine.sent()
     when(gathers_next, after.sent)
 
@@ -425,7 +425,6 @@
     when(depth < DEPTH - 1, lambda: plane_up().wait_send())
     when((core == 0) & (depth > 0), lambda: shard_down().wait_send())
     every_part.wait_send()
-    put.wait()
 
 
 def shards(grad_out, volume, weight):
@@ -433,14 +432,11 @@
     in_vmem = pl.BlockSpec(memory_space=pltpu.VMEM)
     dma = pltpu.SemaphoreType.DMA
     plane = pltpu.VMEM((CHAN, 16, 16, COLS), BF16)
-    return pl.pallas_call(
+    input_grad, kernel_grad = pl.pallas_call(
         body,
-        out_shape=(
-            jax.ShapeDtypeStruct(volume.shape, BF16),
-            jax.ShapeDtypeStruct((27, CI, 4), F32),
-        ),
+        out_shape=(pltpu.VMEM(volume.shape, BF16), pltpu.VMEM((CI, 4, 27), F32)),
         in_specs=[any_space, any_space, any_space],
-        out_specs=(any_space, in_vmem),
+        out_specs=(in_vmem, in_vmem),
         scratch_shapes=[
             plane,
             plane,
@@ -451,7 +447,6 @@
             pltpu.VMEM(weight.shape, BF16),
             pltpu.VMEM((16, 2, 4, 128), F32),
             pltpu.VMEM((DEPTH - 1, 4, 128), F32),
-            pltpu.VMEM(volume.shape, BF16),
             dma((CHAN,)),
             dma((CHAN,)),
             dma,
@@ -466,6 +461,7 @@
         ],
         compiler_params=pltpu.CompilerParams(collective_id=0, has_side_effects=True),
     )(grad_out, volume, weight)
+    return input_grad, jnp.transpose(kernel_grad, (2, 0, 1))
 
 
 def solution(mesh):

time: 44 us -> 41.7 us (0.948)
  local copies, waits for them, and re-layouts: 3.17 us -> 1.3 us
    pallas_call x1 -> x0, local copies, waits for them, and re-layouts: 1.51 us -> none  [shards(): pl.pallas_call(body, out_shape=(jax.ShapeDtypeStruct(volume.shape, BF16),...]
    unnamed x1 -> x2, local copies, waits for them, and re-layouts: 1.67 us -> 1.3 us
where the time goes in v4:
time: 41.7 us; the launch traced here: 41.5 us
  Pallas kernels  39.6 us (95%)
  local copies, waits for them, and re-layouts  1.3 us (3%)
  between operations  0.64 us (2%)
    pallas_call x1, Pallas kernels, shards(): pl.pallas_call(body, out_shape=(pltpu.VMEM(volume.shape, BF16), pltpu.VME...  39.6 us
    unnamed x2, local copies, waits for them, and re-layouts  1.3 us

profile of v4, /device:TPU:1, one launch (start us, length us, event | category | flops | bytes accessed | tf_op | source)
XLA Modules:
  0.0 41.5 jit_solution(1251886888302944448)
XLA Ops:
  0.6 39.6 %shard_map.50 = (bf16[4,2,64,256]{3,2,1,0:T(8,128)(2,1)S(1)}, f32[4,4,27]{2,1,0:T(4,128)S(1)}) custom-call(bf16[8,1,32,128]{3,2,1,0:T(8,128)(2,1)} %grad_hbm.1, bf16[4,2,64,256]{3,2,1,0:T(8,128)(2,1)} %volume_hbm.1, bf16[27,64,128]{2,1,0:T(8,128)(2,1)} %weight_hbm.1), custom_call_target="tpu_custom_call" | custom-call | tf_op jit(solution)/shard_map/pallas_call | solution.py:435
  40.2 0.7 %copy.7 = bf16[4,2,64,256]{3,2,1,0:T(8,128)(2,1)} copy(bf16[4,2,64,256]{3,2,1,0:T(8,128)(2,1)S(1)} %get-tuple-element.6) | data formatting | bytes 524288
  40.9 0.6 %copy.8 = f32[27,4,4]{0,2,1:T(4,128)} copy(f32[27,4,4]{0,2,1:T(4,128)S(1)} %bitcast.1) | data formatting | bytes 3456

commit v5 on v4

--- a/solution.py
+++ b/solution.py
@@ -159,7 +159,7 @@
     grad_hbm, volume_hbm, weight_hbm, result, kernel_ref,
     own, nxt, views, grad, volume, halo, weight, parts, arrived,
     recv_own, recv_next, recv_halo, recv_parts,
-    send_x, send_z, send_chip, send_halo, send_parts, local, know,
+    send_plane, send_chip, send_halo, send_parts, local, know,
 ):
     depth, chan = lax.axis_index("depth"), lax.axis_index("chan")
     core, zh, y = depth % 2, (depth // 2) % 4, depth // 8
@@ -178,6 +178,12 @@
     here = tuple(v * NX + x for v in row)
     others = tuple(tuple(v * NX + c for c in (xl, xr, x2)) for v in row)
 
+    far = (depth, zl * NX + x2)
+    row = (zl, zl + 1 - 2 * (zl % 2), (zl + 2) % NZL, NZL - 1 - zl)
+    column = tuple((depth, v * NX + x) for v in row)
+    here = tuple(v * NX + x for v in row)
+    others = tuple(tuple(v * NX + c for c in (xl, xr, x2)) for v in row)
+
     def up(n):
         return at(x, y, (z + n) % NZ, core), at(x, y, (z + NZ - n) % NZ, core)
 
@@ -197,57 +203,74 @@
     take_grad.start()
     above, below = ((depth + 1) % DEPTH, chan), ((depth + DEPTH - 1) % DEPTH, chan)
     has_above, has_below = depth < DEPTH - 1, depth > 0
+
     calls_above, calls_below = (core == 1) & (zh < 3), (core == 0) & (zh == 0) & has_below
     heard_below, heard_above = (core == 0) & (zh > 0), (core == 1) & (zh == 3) & has_above
-    greets_up, greets_down = (zl == 3) & (zh < 3), z == 0
-    heard_down, heard_up = (zl == 0) & (zh > 0), z == NZ - 1
+
+    def plane_mates(ys):
+        return [((y_ * 4 + zh) * 2 + core_, chan) for y_ in ys for core_ in range(2)]
+
+    def across_groups(zh_):
+        return at(x, y, zh_ * NZL + zl, core)
+
+    def greet_all(devices, sem=barrier):
+        for device in devices:
+            greet(device, sem)
+
+    for y_, later in ((0, (1, 3, 2)), (1, (3, 2)), (3, (2,))):
+        when(y == y_, greet_all, plane_mates(later))
     when(calls_above, greet, above)
     when(calls_below, greet, below)
-    when(greets_up, greet, up(1)[0])
-    when(greets_down, greet, up(1)[1])
-    when(y != 2, greet, at(x, y + 1 - 2 * (y // 3), z, core))
-    when(y == 0, greet, beside[1])
+    when(zh == 0, greet_all, [across_groups(1), across_groups(3)])
+    when(zh == 1, greet, across_groups(2))
+    y_rank = jnp.where(y == 2, 3, jnp.where(y == 3, 2, y))
     take_volume = pltpu.make_async_copy(volume_hbm, volume, local.at[0])
     take_weight = pltpu.make_async_copy(weight_hbm, weight, local.at[1])
     take_volume.start()
     take_weight.start()
     take_grad.wait()
     own[chan] = packed_shard(grad[...].reshape(8, ROWS, COLS))
-    greeted = 7 + jnp.where(heard_down | heard_up, 1, 0)
-    greeted = greeted + jnp.where(y == 2, 2, y % 2) + jnp.where(heard_below | heard_above, 1, 0)
+    greeted = 7 + 2 * y_rank + jnp.minimum(zh, 1) + jnp.where(heard_below | heard_above, 1, 0)
     pl.semaphore_wait(barrier, greeted)
 
     class Plane:
-        def __init__(self, ref, recv, n):
-            self.ref, self.recv, self.n = ref, recv, n
-
-        def copy(self, slot, device, sem):
+        def __init__(self, ref, recv, sem, each):
+            self.ref, self.recv, self.sem, self.each = ref, recv, sem, each
+
+        def copy(self, slot, device):
             return pltpu.make_async_remote_copy(
-                self.ref.at[slot], self.ref.at[slot], sem.at[self.n], self.recv.at[slot],
+                self.ref.at[slot], self.ref.at[slot], self.sem, self.recv.at[slot],
                 device_id=device, device_id_type=MESH,
             )
 
         def sides(self, slot):
             for device in (far, right, left):
-                self.copy(slot, device, send_x).start()
+                self.copy(slot, device).start()
 
         def begin(self):
             self.sides(chan)
-            for k in range(1, 4):
-                self.copy(chan, column[k], send_z).start()
+            for k in (1, 3, 2):
+                self.copy(chan, column[k]).start()
+            self.each(chan)
 
         def wait(self, slot):
-            self.copy(slot, partner, send_x).wait_recv()
-
-        def drained(self, sem, count):
-            shards_ = self.ref.at[pl.ds(0, count)]
+            self.copy(slot, partner).wait_recv()
+            self.each(slot)
+
+        def column_of(self, k):
+            self.copy(here[k], partner).wait_recv()
+            self.sides(here[k])
+            self.each(here[k])
+
+        def rest_of(self, k):
+            for slot in others[k]:
+                self.wait(slot)
+
+        def sent(self):
+            shards_ = self.ref.at[pl.ds(0, CHAN - 1)]
             pltpu.make_async_remote_copy(
-                shards_, shards_, sem.at[self.n], self.recv.at[0], device_id=partner, device_id_type=MESH
+                shards_, shards_, self.sem, self.recv.at[0], device_id=partner, device_id_type=MESH
             ).wait_send()
-
-        def sent(self):
-            self.drained(send_x, 12)
-            self.drained(send_z, 3)
 
     def to_partner(slot):
         return pltpu.make_async_remote_copy(
@@ -258,17 +281,8 @@
     def hand(slot):
         when(core == 1, lambda: to_partner(slot).start())
 
-    mine, after = Plane(own, recv_own, 0), Plane(nxt, recv_next, 1)
-
-    def row_at(k):
-        mine.wait(here[k])
-        mine.sides(here[k])
-        hand(here[k])
-
-    def rest_of(k):
-        for slot in others[k]:
-            mine.wait(slot)
-            hand(slot)
+    mine = Plane(own, recv_own, send_plane.at[0], hand)
+    after = Plane(nxt, recv_next, send_plane.at[1], lambda slot: None)
 
     def plane_up():
         return pltpu.make_async_remote_copy(
@@ -282,80 +296,81 @@
             device_id=((depth + DEPTH - 1) % DEPTH, chan), device_id_type=MESH,
         )
 
-    def tell(n, *devices):
-        for device in devices:
-            greet(device, know.at[n])
-
-    def hear(n, count=2):
-        pl.semaphore_wait(know.at[n], count)
-
-    def neighbours():
-        when(greets_up | greets_down, hear, 0, 1)
-        when(y == 0, hear, 7, 2)
-        when(y % 2 == 1, hear, 7, 1)
-        tell(1, *up(1))
-
-    def two_away():
-        hear(1)
-        tell(2, *up(2))
-
-    def four_away():
-        hear(2)
-        tell(3, partner)
-        hear(3, 1)
-        tell(4, *beside)
-
-    def next_row():
-        hear(4)
-        tell(5, *up(4))
-
-    def all_rows():
-        hear(5)
-        tell(6, *beside)
-
     def trade_down():
-        hear(8, 1)
+        pl.semaphore_wait(know.at[1], 1)
         shard_down().start()
 
     def trade_up():
-        hear(8, 1)
+        pl.semaphore_wait(know.at[1], 1)
         plane_up().start()
 
     def next_rows():
         shard_down().wait_recv()
         after.begin()
-        for k in range(1, 4):
-            after.wait(here[k])
-            after.sides(here[k])
+        for k in (1, 3, 2):
+            after.column_of(k)
+
+    def tell(zh_, n):
+        greet(across_groups(zh_), know.at[n])
+
+    def hear(*semaphores):
+        for n in semaphores:
+            pl.semaphore_wait(know.at[n], 1)
+
+    def whole_plane():
+        when(y != 2, lambda: pl.semaphore_wait(know.at[0], 2 * (3 - y_rank)))
+        for zh_, earlier in ((1, 0), (2, 1), (3, 0)):
+            when(zh == zh_, tell, earlier, 2 + zh_)
+
+    def first_news():
+        @pl.when(zh == 0)
+        def _():
+            hear(3, 5)
+            tell(1, 2)
+
+        @pl.when(zh == 1)
+        def _():
+            hear(4)
+            tell(0, 4)
+
+    def last_news():
+        @pl.when(zh == 0)
+        def _():
+            hear(4)
+            tell(3, 2)
+
+        @pl.when(zh == 1)
+        def _():
+            hear(2)
+            tell(2, 2)
+
+    def trade():
+        when(heard_above, lambda: plane_up().start())
+        when(calls_above, trade_up)
 
     late, early = zh > 0, zh == 0
     gathers_next = (core == 1) & has_above
     mine.begin()
-    hand(chan)
     when(core == 0, lambda: plane_up().start())
-    when(heard_below, tell, 8, below)
-    when(heard_above, tell, 8, above)
-    when(heard_down, tell, 0, up(1)[1])
-    when(heard_up, tell, 0, up(1)[0])
-    when(y % 2 == 1, tell, 7, at(x, 0, z, core))
-    when(y == 2, tell, 7, *beside)
-    when(heard_below, lambda: shard_down().start())
-    row_at(1)
-    when(late, neighbours)
-    row_at(2)
-    when(late, two_away)
-    row_at(3)
-    when(early, neighbours)
+    when(heard_below & (zh == 1), lambda: shard_down().start())
+    when(heard_below, greet, below, know.at[1])
+    when(heard_above, greet, above, know.at[1])
+    for y_, sooner in ((1, (0,)), (3, (0, 1)), (2, (0, 1, 3))):
+        when(y == y_, greet_all, plane_mates(sooner), know.at[0])
+    whole_plane()
+    mine.column_of(1)
+    mine.rest_of(0)
+    mine.column_of(3)
+    mine.column_of(2)
+    when(late, trade)
+    when(heard_below & (zh > 1), lambda: shard_down().start())
     take_volume.wait()
     own_views(volume, views)
-    when(heard_above, lambda: plane_up().start())
-    when(calls_above, trade_up)
-    when(early, two_away)
-    four_away()
+    when(early, trade)
     when(calls_below, trade_down)
-    rest_of(0)
-    next_row()
-    rest_of(1)
+    first_news()
+    mine.rest_of(1)
+    last_news()
     when(has_below, lambda: plane_up().wait_recv())
 
     @pl.when(depth == 0)
@@ -363,14 +378,13 @@
         halo[...] = jnp.zeros_like(halo)
 
     halo_views(halo, views)
-    when(gathers_next & (zh < 2), next_rows)
-    rest_of(2)
-    all_rows()
-    rest_of(3)
+    when(gathers_next & early, next_rows)
+    mine.rest_of(2)
+    mine.rest_of(3)
     terms = kernel_terms(own, views)
     parts[:, 0] = terms[:, :4]
     parts[:, 1] = terms[:, 4:]
-    hear(6)
+    when(zh > 1, hear, 2)
     for step in FAR_FIRST:
         dy, dz, dc = step // 8, (step // 2) % 4, step % 2
         peer = (((y + dy) % NY) * 4 + (zh + dz) % 4) * 2 + (core + dc) % 2
@@ -381,13 +395,12 @@
 
     take_weight.wait()
     for_own, for_next = own_weights(weight, chan)
-    when(gathers_next & (zh >= 2), next_rows)
+    when(gathers_next & late, next_rows)
 
     @pl.when(gathers_next)
     def _():
         for k in range(4):
-            for slot in others[k]:
-                after.wait(slot)
+            after.rest_of(k)
 
     @pl.when(depth == DEPTH - 1)
     def _():
@@ -452,12 +465,11 @@
             dma,
             dma,
             dma((2,)),
-            dma((2,)),
             dma,
             dma((2,)),
             dma,
             dma((4,)),
-            pltpu.SemaphoreType.REGULAR((9,)),
+            pltpu.SemaphoreType.REGULAR((6,)),
         ],
         compiler_params=pltpu.CompilerParams(collective_id=0, has_side_effects=True),
     )(grad_out, volume, weight)

time: 41.7 us -> 40.1 us (0.962)
  Pallas kernels: 39.6 us -> 38.1 us
    pallas_call x1, Pallas kernels: 39.6 us -> 38.1 us  [shards(): pl.pallas_call(body, out_shape=(pltpu.VMEM(volume.shape, BF16), pltpu.VME...]
where the time goes in v5:
time: 40.1 us; the launch traced here: 40 us
  Pallas kernels  38.1 us (95%)
  local copies, waits for them, and re-layouts  1.3 us (3%)
  between operations  0.64 us (2%)
    pallas_call x1, Pallas kernels, shards(): pl.pallas_call(body, out_shape=(pltpu.VMEM(volume.shape, BF16), pltpu.VME...  38.1 us
    unnamed x2, local copies, waits for them, and re-layouts  1.3 us

profile of v5, /device:TPU:1, one launch (start us, length us, event | category | flops | bytes accessed | tf_op | source)
XLA Modules:
  0.0 40.0 jit_solution(4309968460416151304)
XLA Ops:
  0.6 38.1 %shard_map.50 = (bf16[4,2,64,256]{3,2,1,0:T(8,128)(2,1)S(1)}, f32[4,4,27]{2,1,0:T(4,128)S(1)}) custom-call(bf16[8,1,32,128]{3,2,1,0:T(8,128)(2,1)} %grad_hbm.1, bf16[4,2,64,256]{3,2,1,0:T(8,128)(2,1)} %volume_hbm.1, bf16[27,64,128]{2,1,0:T(8,128)(2,1)} %weight_hbm.1), custom_call_target="tpu_custom_call" | custom-call | tf_op jit(solution)/shard_map/pallas_call | solution.py:448
  38.7 0.7 %copy.7 = bf16[4,2,64,256]{3,2,1,0:T(8,128)(2,1)} copy(bf16[4,2,64,256]{3,2,1,0:T(8,128)(2,1)S(1)} %get-tuple-element.6) | data formatting | bytes 524288
  39.4 0.6 %copy.8 = f32[27,4,4]{0,2,1:T(4,128)} copy(f32[27,4,4]{0,2,1:T(4,128)S(1)} %bitcast.1) | data formatting | bytes 3456

commit v6 on v5

--- a/solution.py
+++ b/solution.py
@@ -12,6 +12,7 @@
 F32 = jnp.float32
 NX, NY, NZ, NZL, DEPTH, CHAN = 4, 4, 16, 4, 32, 16
 CI, ROWS, COLS = 4, 32, 128
+CUT = 8
 FAR_FIRST = sorted(range(1, 32), key=lambda n: -(4 * min(n // 2 % 4, 4 - n // 2 % 4) + min(n // 8, 4 - n // 8)))
 
 
@@ -233,19 +234,27 @@
     greeted = 7 + 2 * y_rank + jnp.minimum(zh, 1) + jnp.where(heard_below | heard_above, 1, 0)
     pl.semaphore_wait(barrier, greeted)
 
+    odd = zl % 2 == 1
+
     class Plane:
         def __init__(self, ref, recv, sem, each):
             self.ref, self.recv, self.sem, self.each = ref, recv, sem, each
 
-        def copy(self, slot, device):
+        def piece(self, slot, part):
+            if part == 0:
+                return self.ref.at[slot]
+            return self.ref.at[slot, pl.ds(0, CUT)] if part == 1 else self.ref.at[slot, pl.ds(CUT, 16 - CUT)]
+
+        def copy(self, slot, device, part=0):
+            piece = self.piece(slot, part)
             return pltpu.make_async_remote_copy(
-                self.ref.at[slot], self.ref.at[slot], self.sem, self.recv.at[slot],
+                piece, piece, self.sem.at[part], self.recv.at[2 * slot + part // 2],
                 device_id=device, device_id_type=MESH,
             )
 
-        def sides(self, slot):
+        def sides(self, slot, part=0):
             for device in (far, right, left):
-                self.copy(slot, device).start()
+                self.copy(slot, device, part).start()
 
         def begin(self):
             self.sides(chan)
@@ -253,28 +262,46 @@
                 self.copy(chan, column[k]).start()
             self.each(chan)
 
-        def wait(self, slot):
-            self.copy(slot, partner).wait_recv()
-            self.each(slot)
+        def wait(self, slot, *parts_):
+            for part in parts_ or (0,):
+                self.copy(slot, partner, part).wait_recv()
+
+        def nearest(self):
+            self.wait(here[1])
+            self.sides(here[1], 2)
+            when(odd, self.sides, here[1], 1)
+            self.each(here[1])
+
+        def own_row(self):
+            for slot in others[0]:
+                self.wait(slot)
+                when(odd, lambda slot=slot: self.copy(slot, column[1], 1).start())
+                self.each(slot)
 
         def column_of(self, k):
-            self.copy(here[k], partner).wait_recv()
+            self.wait(here[k])
             self.sides(here[k])
             self.each(here[k])
 
         def rest_of(self, k):
             for slot in others[k]:
-                self.wait(slot)
+                self.wait(slot, *((1, 2) if k == 1 else ()))
+                self.each(slot)
+
+        def drained(self, count, part):
+            pieces = self.piece(pl.ds(0, count), part)
+            pltpu.make_async_remote_copy(
+                pieces, pieces, self.sem.at[part], self.recv.at[0], device_id=partner, device_id_type=MESH
+            ).wait_send()
 
         def sent(self):
-            shards_ = self.ref.at[pl.ds(0, CHAN - 1)]
-            pltpu.make_async_remote_copy(
-                shards_, shards_, self.sem, self.recv.at[0], device_id=partner, device_id_type=MESH
-            ).wait_send()
+            self.drained(12, 0)
+            self.drained(3, 2)
+            when(odd, self.drained, 6, 1)
 
     def to_partner(slot):
         return pltpu.make_async_remote_copy(
-            own.at[slot], nxt.at[slot], send_chip, recv_next.at[slot],
+            own.at[slot], nxt.at[slot], send_chip, recv_next.at[2 * slot],
             device_id=partner, device_id_type=MESH,
         )
 
@@ -292,7 +319,7 @@
 
     def shard_down():
         return pltpu.make_async_remote_copy(
-            own.at[chan], nxt.at[chan], send_halo.at[1], recv_next.at[chan],
+            own.at[chan], nxt.at[chan], send_halo.at[1], recv_next.at[2 * chan],
             device_id=((depth + DEPTH - 1) % DEPTH, chan), device_id_type=MESH,
         )
 
@@ -307,8 +334,10 @@
     def next_rows():
         shard_down().wait_recv()
         after.begin()
-        for k in (1, 3, 2):
-            after.column_of(k)
+        after.nearest()
+        after.own_row()
+        after.column_of(3)
+        after.column_of(2)
 
     def tell(zh_, n):
         greet(across_groups(zh_), know.at[n])
@@ -358,8 +387,8 @@
     for y_, sooner in ((1, (0,)), (3, (0, 1)), (2, (0, 1, 3))):
         when(y == y_, greet_all, plane_mates(sooner), know.at[0])
     whole_plane()
-    mine.column_of(1)
-    mine.rest_of(0)
+    mine.nearest()
+    mine.own_row()
     mine.column_of(3)
     mine.column_of(2)
     when(late, trade)
@@ -370,6 +399,7 @@
     when(calls_below, trade_down)
     first_news()
     mine.rest_of(1)
+    when(gathers_next & early, next_rows)
     last_news()
     when(has_below, lambda: plane_up().wait_recv())
 
@@ -378,7 +408,6 @@
         halo[...] = jnp.zeros_like(halo)
 
     halo_views(halo, views)
-    when(gathers_next & early, next_rows)
     mine.rest_of(2)
     mine.rest_of(3)
     terms = kernel_terms(own, views)
@@ -399,7 +428,7 @@
 
     @pl.when(gathers_next)
     def _():
-        for k in range(4):
+        for k in range(1, 4):
             after.rest_of(k)
 
     @pl.when(depth == DEPTH - 1)
@@ -460,11 +489,11 @@
             pltpu.VMEM(weight.shape, BF16),
             pltpu.VMEM((16, 2, 4, 128), F32),
             pltpu.VMEM((DEPTH - 1, 4, 128), F32),
-            dma((CHAN,)),
-            dma((CHAN,)),
+            dma((2 * CHAN,)),
+            dma((2 * CHAN,)),
             dma,
             dma,
-            dma((2,)),
+            dma((2, 3)),
             dma,
             dma((2,)),
             dma,

time: 40.1 us -> 40.1 us (level)
  no operation moved by 1% of the time
where the time goes in v6:
time: 40.1 us; the launch traced here: 39.9 us
  Pallas kernels  38 us (95%)
  local copies, waits for them, and re-layouts  1.3 us (3%)
  between operations  0.64 us (2%)
    pallas_call x1, Pallas kernels, shards(): pl.pallas_call(body, out_shape=(pltpu.VMEM(volume.shape, BF16), pltpu.VME...  38 us
    unnamed x2, local copies, waits for them, and re-layouts  1.3 us

profile of v6, /device:TPU:1, one launch (start us, length us, event | category | flops | bytes accessed | tf_op | source)
XLA Modules:
  0.0 39.9 jit_solution(11133658575235342925)
XLA Ops:
  0.6 38.0 %shard_map.50 = (bf16[4,2,64,256]{3,2,1,0:T(8,128)(2,1)S(1)}, f32[4,4,27]{2,1,0:T(4,128)S(1)}) custom-call(bf16[8,1,32,128]{3,2,1,0:T(8,128)(2,1)} %grad_hbm.1, bf16[4,2,64,256]{3,2,1,0:T(8,128)(2,1)} %volume_hbm.1, bf16[27,64,128]{2,1,0:T(8,128)(2,1)} %weight_hbm.1), custom_call_target="tpu_custom_call" | custom-call | tf_op jit(solution)/shard_map/pallas_call | solution.py:477
  38.6 0.7 %copy.7 = bf16[4,2,64,256]{3,2,1,0:T(8,128)(2,1)} copy(bf16[4,2,64,256]{3,2,1,0:T(8,128)(2,1)S(1)} %get-tuple-element.6) | data formatting | bytes 524288
  39.3 0.6 %copy.8 = f32[27,4,4]{0,2,1:T(4,128)} copy(f32[27,4,4]{0,2,1:T(4,128)S(1)} %bitcast.1) | data formatting | bytes 3456

commit v7 on v6

--- a/solution.py
+++ b/solution.py
@@ -389,9 +389,10 @@
     whole_plane()
     mine.nearest()
     mine.own_row()
+    when(zh == 1, trade)
     mine.column_of(3)
     mine.column_of(2)
-    when(late, trade)
+    when(zh > 1, trade)
     when(heard_below & (zh > 1), lambda: shard_down().start())
     take_volume.wait()
     own_views(volume, views)
@@ -467,6 +468,17 @@
     when(depth < DEPTH - 1, lambda: plane_up().wait_send())
     when((core == 0) & (depth > 0), lambda: shard_down().wait_send())
     every_part.wait_send()
+
+
+def finish(result, sums, input_hbm, kernel_hbm, sems):
+    puts = [
+        pltpu.make_async_copy(result, input_hbm, sems.at[0]),
+        pltpu.make_async_copy(sums, kernel_hbm, sems.at[1]),
+    ]
+    for put in puts:
+        put.start()
+    for put in puts:
+        put.wait()
 
 
 def shards(grad_out, volume, weight):
@@ -502,6 +514,16 @@
         ],
         compiler_params=pltpu.CompilerParams(collective_id=0, has_side_effects=True),
     )(grad_out, volume, weight)
+    input_grad, kernel_grad = pl.pallas_call(
+        finish,
+        out_shape=(jax.ShapeDtypeStruct(volume.shape, BF16), jax.ShapeDtypeStruct((CI, 4, 27), F32)),
+        in_specs=[in_vmem, in_vmem],
+        out_specs=(any_space, any_space),
+        scratch_shapes=[dma((2,))],
+    )(
+        pltpu.with_memory_space_constraint(input_grad, pltpu.VMEM),
+        pltpu.with_memory_space_constraint(kernel_grad, pltpu.VMEM),
+    )
     return input_grad, jnp.transpose(kernel_grad, (2, 0, 1))
 
 

time: 40.1 us -> 39.3 us (0.980)
  local copies, waits for them, and re-layouts: 1.3 us -> 0 us
  Pallas kernels: 38 us -> 38.5 us
    unnamed x2 -> x0, local copies, waits for them, and re-layouts: 1.3 us -> none
    pallas_call x0 -> x1, Pallas kernels: none -> 0.72 us  [shards(): pl.pallas_call(finish, out_shape=(jax.ShapeDtypeStruct(volume.shape, BF16...]
where the time goes in v7:
time: 39.3 us; the launch traced here: 39.1 us
  Pallas kernels  38.5 us (98%)
  between operations  0.64 us (2%)
    pallas_call x1, Pallas kernels, shards(): pl.pallas_call(body, out_shape=(pltpu.VMEM(volume.shape, BF16), pltpu.VME...  37.8 us

profile of v7, /device:TPU:1, one launch (start us, length us, event | category | flops | bytes accessed | tf_op | source)
XLA Modules:
  0.0 39.1 jit_solution(5528318766467271575)
XLA Ops:
  0.6 37.8 %shard_map.50 = (bf16[4,2,64,256]{3,2,1,0:T(8,128)(2,1)S(1)}, f32[4,4,27]{2,1,0:T(4,128)S(1)}) custom-call(bf16[8,1,32,128]{3,2,1,0:T(8,128)(2,1)} %grad_hbm.1, bf16[4,2,64,256]{3,2,1,0:T(8,128)(2,1)} %volume_hbm.1, bf16[27,64,128]{2,1,0:T(8,128)(2,1)} %weight_hbm.1), custom_call_target="tpu_custom_call" | custom-call | tf_op jit(solution)/shard_map/pallas_call | solution.py:489
  38.4 0.7 %shard_map.51 = (bf16[4,2,64,256]{3,2,1,0:T(8,128)(2,1)}, f32[4,4,27]{2,1,0:T(4,128)}) custom-call(bf16[4,2,64,256]{3,2,1,0:T(8,128)(2,1)S(1)} %get-tuple-element.6.result, f32[4,4,27]{2,1,0:T(4,128)S(1)} %get-tuple-element.7.sums), custom_call_target="tpu_custom_call" | custom-call | tf_op jit(solution)/shard_map/pallas_call | solution.py:517

commit v8 on v7

--- a/solution.py
+++ b/solution.py
@@ -83,7 +83,7 @@
     c, t = k >> 5, k & 31
     a, b, e = t // 9, (t // 3) % 3, t % 3
     source = jnp.where(a > 0, 16 * (3 * a - 3 + e) + 4 * b, jnp.where(b < 2, 16 * (3 * b + e) + 12, 96 + 4 * e))
-    return jnp.where((col == source + c) & (t < 27), 1.0, 0.0)
+    return picks((col == source + c) & (t < 27))
 
 
 def own_weights(weight_ref, chan):
@@ -450,9 +450,12 @@
     )
     every_part.wait_recv()
     total = parts[depth // 2, depth % 2] + jnp.sum(arrived[...], axis=0)
-    chosen = jnp.dot(
-        jnp.concatenate([total, total], axis=0), choose, precision=lax.Precision.HIGHEST, preferred_element_type=F32
-    )
+    whole = jnp.concatenate([total, total], axis=0)
+    high = whole.astype(BF16).astype(F32)
+    middle = (whole - high).astype(BF16).astype(F32)
+    split = jnp.concatenate([high, middle, whole - high - middle], axis=0).astype(BF16)
+    chosen = mm(split, choose)
+    chosen = chosen[:8] + chosen[8:16] + chosen[16:]
     chosen = chosen * (1.0 / math.sqrt(DEPTH * ROWS * COLS))
     for c in range(CI):
         kernel_ref[c] = chosen[:4, 32 * c : 32 * c + 27]

time: 39.3 us -> 39.2 us (level)
  no operation moved by 1% of the time
where the time goes in v8:
time: 39.2 us; the launch traced here: 39.1 us
  Pallas kernels  38.4 us (98%)
  between operations  0.64 us (2%)
    pallas_call x1, Pallas kernels, shards(): pl.pallas_call(body, out_shape=(pltpu.VMEM(volume.shape, BF16), pltpu.VME...  37.7 us

profile of v8, /device:TPU:1, one launch (start us, length us, event | category | flops | bytes accessed | tf_op | source)
XLA Modules:
  0.0 39.1 jit_solution(9481577655347821280)
XLA Ops:
  0.6 37.7 %shard_map.50 = (bf16[4,2,64,256]{3,2,1,0:T(8,128)(2,1)S(1)}, f32[4,4,27]{2,1,0:T(4,128)S(1)}) custom-call(bf16[8,1,32,128]{3,2,1,0:T(8,128)(2,1)} %grad_hbm.1, bf16[4,2,64,256]{3,2,1,0:T(8,128)(2,1)} %volume_hbm.1, bf16[27,64,128]{2,1,0:T(8,128)(2,1)} %weight_hbm.1), custom_call_target="tpu_custom_call" | custom-call | tf_op jit(solution)/shard_map/pallas_call | solution.py:492
  38.3 0.7 %shard_map.51 = (bf16[4,2,64,256]{3,2,1,0:T(8,128)(2,1)}, f32[4,4,27]{2,1,0:T(4,128)}) custom-call(bf16[4,2,64,256]{3,2,1,0:T(8,128)(2,1)S(1)} %get-tuple-element.6.result, f32[4,4,27]{2,1,0:T(4,128)S(1)} %get-tuple-element.7.sums), custom_call_target="tpu_custom_call" | custom-call | tf_op jit(solution)/shard_map/pallas_call | solution.py:520

commit v9 on v8

--- a/solution.py
+++ b/solution.py
@@ -257,9 +257,9 @@
                 self.copy(slot, device, part).start()
 
         def begin(self):
-            self.sides(chan)
             for k in (1, 3, 2):
                 self.copy(chan, column[k]).start()
+            self.sides(chan)
             self.each(chan)
 
         def wait(self, slot, *parts_):

time: 39.2 us -> 39.2 us (level)
  no operation moved by 1% of the time
where the time goes in v9:
time: 39.2 us; the launch traced here: 39 us
  Pallas kernels  38.4 us (98%)
  between operations  0.64 us (2%)
    pallas_call x1, Pallas kernels, shards(): pl.pallas_call(body, out_shape=(pltpu.VMEM(volume.shape, BF16), pltpu.VME...  37.7 us

profile of v9, /device:TPU:1, one launch (start us, length us, event | category | flops | bytes accessed | tf_op | source)
XLA Modules:
  0.0 39.0 jit_solution(10188086839539266656)
XLA Ops:
  0.6 37.7 %shard_map.50 = (bf16[4,2,64,256]{3,2,1,0:T(8,128)(2,1)S(1)}, f32[4,4,27]{2,1,0:T(4,128)S(1)}) custom-call(bf16[8,1,32,128]{3,2,1,0:T(8,128)(2,1)} %grad_hbm.1, bf16[4,2,64,256]{3,2,1,0:T(8,128)(2,1)} %volume_hbm.1, bf16[27,64,128]{2,1,0:T(8,128)(2,1)} %weight_hbm.1), custom_call_target="tpu_custom_call" | custom-call | tf_op jit(solution)/shard_map/pallas_call | solution.py:492
  38.3 0.7 %shard_map.51 = (bf16[4,2,64,256]{3,2,1,0:T(8,128)(2,1)}, f32[4,4,27]{2,1,0:T(4,128)}) custom-call(bf16[4,2,64,256]{3,2,1,0:T(8,128)(2,1)S(1)} %get-tuple-element.6.result, f32[4,4,27]{2,1,0:T(4,128)S(1)} %get-tuple-element.7.sums), custom_call_target="tpu_custom_call" | custom-call | tf_op jit(solution)/shard_map/pallas_call | solution.py:520
